TPU v7x, 512 devices: a whole 4x8x8 slice. The times are simulated.
512 devices in a mesh: member: 32 (over z_hi, y, core), tile: 16 (over z_lo, x).
Axes of the slice: x: 4, y: 8, z: 8 (z_hi: 2, z_lo: 4; z = z_hi * 4 + z_lo), core: 2. Of those that a mesh axis runs over, the one named last changes fastest.
Arguments:
- perturbations: bfloat16 [256, 2, 5, 8, 32, 2048], P('member', None, None, None, None, 'tile'), may hold values from -6 to 6
- gradient_store: float32 [2, 5, 8, 32, 2048], P(None, None, None, 'member', 'tile'), may hold values from -6 to 6
- diffusivity: float32 [8, 32, 2048], P(None, None, 'tile'), may hold values from 0.2 to 0.4
- slab_owner: int32 [32], replicated, may hold values from 0 to 31, each once
Outputs:
- increment_store: float32 [2, 5, 8, 32, 2048], P(None, None, None, 'member', 'tile')
Inputs may be any that keep to these rules, and one draw needn't show every extreme that they name: `slab_owner`: each member index holds exactly one slab.
All inputs are finite; a program needn't handle non-finite values.
Results may differ from a plain program's by a relative error of at most 0.0003.
Values sent between devices are 32-bit elements; how exact they have to be, the bound alone decides.
A program may use at most 128 MiB of HBM per device.

v0:
```python
import jax
import jax.numpy as jnp
from jax import lax
from jax.sharding import PartitionSpec as P

SWEEPS = 10


def extended_2(array, sides, width):
    for axis, dim in sides:
        size, length = (lax.axis_size(axis), array.shape[dim])
        up = [(i, (i + 1) % size) for i in range(size - 1)]
        down = [(j, i) for i, j in up]
        last = lax.slice_in_dim(array, length - width, length, axis=dim)
        initial = lax.slice_in_dim(array, 0, width, axis=dim)
        before = lax.ppermute(last, axis, up)
        after = lax.ppermute(initial, axis, down)
        array = jnp.concatenate([before, array, after], axis=dim)
    return array


def neighbours(grid_field):
    count = grid_field.ndim
    widths_y = [(0, 0)] * (count - 2) + [(1, 1), (0, 0)]
    widths_z = [(0, 0)] * (count - 3) + [(1, 1), (0, 0), (0, 0)]
    padded_y = jnp.pad(grid_field, widths_y)
    padded_z = jnp.pad(grid_field, widths_z)
    return (
        padded_y[..., :-2, :]
        + padded_y[..., 2:, :]
        + padded_z[..., :-2, :, :]
        + padded_z[..., 2:, :, :]
    )


def diffuse(values, coefficient):
    scaled = coefficient * values
    centre = values[..., 1:-1]
    coeff_mid = coefficient[..., 1:-1]
    scaled_mid = scaled[..., 1:-1]
    inflow = scaled[..., :-2] + scaled[..., 2:] + neighbours(scaled_mid)
    outflow = coefficient[..., :-2] + coefficient[..., 2:] + neighbours(coeff_mid)
    return centre + coeff_mid * (inflow - outflow * centre)


def block_rows(slab_owner, slab_rows):
    offsets = jnp.arange(slab_rows, dtype=jnp.int32)
    return (slab_owner[:, None] * slab_rows + offsets[None, :]).reshape(-1)


def body(perturbations, gradient_store, diffusivity, slab_owner):
    members_here = perturbations.shape[0]
    slot_count = perturbations.shape[1]
    var_count = perturbations.shape[2]
    n_member = lax.axis_size("member")
    slab_rows = gradient_store.shape[3]
    norm_factor = 1.0 / (members_here * n_member - 1)
    gathered = lax.all_gather(gradient_store, "member", axis=3, tiled=True)
    gradient = jnp.take(gathered, block_rows(slab_owner, slab_rows), axis=3)
    weighted = None
    for slot in range(slot_count):
        for var_index in range(var_count):
            term = (
                perturbations[:, slot, var_index].astype(jnp.float32)
                * gradient[slot, var_index][None]
            )
            weighted = term if weighted is None else weighted + term
    coeff_ext = extended_2(diffusivity, (("tile", 2),), 1)

    def one_sweep(sweep_index, field_state):
        extended = extended_2(field_state, (("tile", 3),), 1)
        return diffuse(extended, coeff_ext)

    local_field = lax.fori_loop(0, SWEEPS, one_sweep, weighted)
    term_list = []
    for slot in range(slot_count):
        var_list = []
        for var_index in range(var_count):
            var_list.append(
                jnp.sum(perturbations[:, slot, var_index].astype(jnp.float32) * local_field, axis=0)
            )
        term_list.append(jnp.stack(var_list, axis=0))
    member_terms = jnp.stack(term_list, axis=0)
    store_rows = block_rows(jnp.argsort(slab_owner), slab_rows)
    stored_terms = jnp.take(member_terms, store_rows, axis=3)
    summed = lax.psum(stored_terms, "member")
    owned = lax.dynamic_slice_in_dim(summed, lax.axis_index("member") * slab_rows, slab_rows, 3)
    return owned * norm_factor


def solution(mesh):
    in_specs = (
        P("member", None, None, None, None, "tile"),
        P(None, None, None, "member", "tile"),
        P(None, None, "tile"),
        P(),
    )
    out_specs = P(None, None, None, "member", "tile")
    return jax.shard_map(body, mesh=mesh, in_specs=in_specs, out_specs=out_specs, check_vma=False)
```

profile of v0, /device:TPU:6, one launch (start us, length us, event | category | flops | bytes accessed | tf_op | source)
XLA Modules:
  0.0 747.9 jit_solution(2813041050299752099)
XLA Ops:
  9.0 4.2 collective-permute-start.2
  17.1 5.2 fusion.31
  26.1 2.9 copy.150
  29.0 2.9 copy.151
  34.7 2.8 copy.153
  37.5 2.9 copy.154
  40.4 2.9 copy.155
  43.3 2.9 copy.156
  52.0 51.2 %all-gather.2.cloned.1.call-done = f32[2,5,8,32,128]{4,2,3,1,0:T(8,128)} async-done(((f32[2,5,8,1,128]{4,2,3,1,0:T(8,128)}), f32[2,5,8,32,128]{4,2,3,1,0:T(8,128)}) %all-gather.2.cloned.1.call-update) | async-done | bytes 1310736 | tf_op jit(solution)/shard_map/all_gather | solution.py:58
  103.2 3.1 gather_fusion
  124.5 11.8 %fusion.18 = f32[8,8,32,128]{2,1,3,0:T(8,128)} fusion(bf16[8,1,1,8,32,128]{4,3,5,0,2,1:T(8,128)(2,1)} %copy.158, bf16[8,1,1,8,32,128]{4,3,5,0,2,1:T(8,128)(2,1)} %copy.157, bf16[8,1,1,8,32,128]{4,3,5,0,2,1:T(8,128)(2,1)} %copy.156, bf16[8,1,1,8,32,128]{4,3,5,0,2,1:T(8,128)(2,1)} %copy.155, bf16[8,1,1,8,32,128]{4,3,5,0,2,1:T(8,128)(2,1)} %copy.154, ...), kind=kLoop, calls=%fused_computation.48 | loop fusion | flops 7602176 | bytes 7602176 | tf_op jit(solution)/shard_map/add | solution.py:67
  136.2 235.7 %while.12 = (s32[]{:T(128)}, f32[8,8,32,128]{2,1,3,0:T(8,128)}, f32[8,32,128]{1,0,2:T(8,128)}, f32[8,32,130]{1,0,2:T(8,128)}, f32[8,32,128]{1,0,2:T(8,128)S(1)}, /*index=5*/s32[]{:T(128)}) while((s32[]{:T(128)}, f32[8,8,32,128]{2,1,3,0:T(8,128)}, f32[8,32,128]{1,0,2:T(8,128)}, f32[8,32,130]{1,0,2:T(8,128)}, f32[8,32,128]{1,0,2:T(8,128)S(1)}, ...), condition=%wide.region_1.3_spmd, body=%wide.region_0.0_spmd.sunk | while | flops 3289090 | bytes 16947432 | solution.py:74
  140.1 5.2 collective-permute-start.1
  162.8 6.0 collective-permute-start.1
  186.3 6.0 collective-permute-start.1
  209.9 6.0 collective-permute-start.1
  233.4 6.0 collective-permute-start.1
  256.9 6.0 collective-permute-start.1
  280.5 6.0 collective-permute-start.1
  304.0 6.0 collective-permute-start.1
  327.6 6.0 collective-permute-start.1
  351.1 6.0 collective-permute-start.1
  371.9 12.9 %fusion.23 = (f32[8,32,128]{1,0,2:T(8,128)S(1)}, f32[8,32,128]{1,0,2:T(8,128)S(1)}, f32[8,32,128]{1,0,2:T(8,128)S(1)}, f32[8,32,128]{1,0,2:T(8,128)S(1)}, f32[8,...) fusion(f32[8,8,32,128]{2,1,3,0:T(8,128)} %get-tuple-element.66,, ...), kind=kLoop, calls=%fused_computation.53 | loop fusion | flops 7536640 | bytes 7602176 | tf_op jit(solution)/shard_map/reduce_sum | solution.py:80
  399.1 340.6 %all-reduce.6.cloned.1.call-done = f32[2,5,8,32,128]{4,2,1,0,3:T(8,128)} async-done(((f32[2,5,8,32,128]{4,2,1,0,3:T(8,128)}), f32[2,5,8,32,128]{4,2,1,0,3:T(8,128)}) %all-reduce.6.cloned.1.call-update) | async-done | bytes 1310736 | tf_op jit(solution)/shard_map/psum | solution.py:86
  (277 shorter events, 227.8 us)
Async XLA Ops:
  6.5 96.6 %all-gather.2.cloned.1.call-start = ((), (), s32[]{:S(2)}) async-start(), calls=%async_computation | async-start | bytes 1351680 | tf_op jit(solution)/shard_map/all_gather | solution.py:58
  7.3 732.4 %all-reduce.6.cloned.1.call-start = ((), (), s32[]{:S(2)}) async-start(), calls=%async_computation.1 | async-start | bytes 2621440 | tf_op jit(solution)/shard_map/psum | solution.py:86
  9.0 41.2 %collective-permute-start.2 = (f32[8,32,1]{2,1,0:T(8,128)}, f32[8,32,1]{2,1,0:T(8,128)S(1)}, u32[]{:S(2)}, u32[]{:S(2)}) collective-permute-start(f32[8,32,1]{2,1,0:T(8,128)} %get-tuple-element.125), channel_id=1, source_target_pairs={{0,1},{1,2},{2,3},{3,4},{4,5},{5,6},{6,7},{7,8},{8,9},{9,10},{10,1... | collective-permute-start | bytes 3080 | tf_op jit(solution)/shard_map/ppermute | solution.py:16
  13.2 37.0 %collective-permute-start.3 = (f32[8,32,1]{2,1,0:T(8,128)}, f32[8,32,1]{2,1,0:T(8,128)S(1)}, u32[]{:S(2)}, u32[]{:S(2)}) collective-permute-start(f32[8,32,1]{2,1,0:T(8,128)} %get-tuple-element.126), channel_id=1, source_target_pairs={{1,0},{2,1},{3,2},{4,3},{5,4},{6,5},{7,6},{8,7},{9,8},{10,9},{11,1... | collective-permute-start | bytes 3080 | tf_op jit(solution)/shard_map/ppermute | solution.py:17
  137.3 16.5 %collective-permute-start = (f32[8,8,32,1]{2,1,3,0:T(8,128)S(1)}, f32[8,8,32,1]{2,1,3,0:T(8,128)S(1)}, u32[]{:S(2)}, u32[]{:S(2)}) collective-permute-start(f32[8,8,32,1]{2,1,3,0:T(8,128)S(1)} %get-tuple-element.160), channel_id=1, source_target_pairs={{1,0},{2,1},{3,2},{4,3},{5,4},{6,5},{7,6},{8,7},{9,8},{10,9},{11,1... | collective-permute-start | bytes 24584 | tf_op jit(solution)/shard_map/while/body/eval_jaxpr/ppermute | solution.py:17
  140.1 14.2 %collective-permute-start.1 = (f32[8,8,32,1]{2,1,3,0:T(8,128)S(1)}, f32[8,8,32,1]{2,1,3,0:T(8,128)}, u32[]{:S(2)}, u32[]{:S(2)}) collective-permute-start(f32[8,8,32,1]{2,1,3,0:T(8,128)S(1)} %get-tuple-element.161), channel_id=1, source_target_pairs={{0,1},{1,2},{2,3},{3,4},{4,5},{5,6},{6,7},{7,8},{8,9},{9,10},{10,1... | collective-permute-start | bytes 24584 | tf_op jit(solution)/shard_map/while/body/eval_jaxpr/ppermute | solution.py:16
  160.8 16.5 %collective-permute-start = (f32[8,8,32,1]{2,1,3,0:T(8,128)S(1)}, f32[8,8,32,1]{2,1,3,0:T(8,128)S(1)}, u32[]{:S(2)}, u32[]{:S(2)}) collective-permute-start(f32[8,8,32,1]{2,1,3,0:T(8,128)S(1)} %get-tuple-element.160), channel_id=1, source_target_pairs={{1,0},{2,1},{3,2},{4,3},{5,4},{6,5},{7,6},{8,7},{9,8},{10,9},{11,1... | collective-permute-start | bytes 24584 | tf_op jit(solution)/shard_map/while/body/eval_jaxpr/ppermute | solution.py:17
  162.8 15.0 %collective-permute-start.1 = (f32[8,8,32,1]{2,1,3,0:T(8,128)S(1)}, f32[8,8,32,1]{2,1,3,0:T(8,128)}, u32[]{:S(2)}, u32[]{:S(2)}) collective-permute-start(f32[8,8,32,1]{2,1,3,0:T(8,128)S(1)} %get-tuple-element.161), channel_id=1, source_target_pairs={{0,1},{1,2},{2,3},{3,4},{4,5},{5,6},{6,7},{7,8},{8,9},{9,10},{10,1... | collective-permute-start | bytes 24584 | tf_op jit(solution)/shard_map/while/body/eval_jaxpr/ppermute | solution.py:16
  184.4 16.5 %collective-permute-start = (f32[8,8,32,1]{2,1,3,0:T(8,128)S(1)}, f32[8,8,32,1]{2,1,3,0:T(8,128)S(1)}, u32[]{:S(2)}, u32[]{:S(2)}) collective-permute-start(f32[8,8,32,1]{2,1,3,0:T(8,128)S(1)} %get-tuple-element.160), channel_id=1, source_target_pairs={{1,0},{2,1},{3,2},{4,3},{5,4},{6,5},{7,6},{8,7},{9,8},{10,9},{11,1... | collective-permute-start | bytes 24584 | tf_op jit(solution)/shard_map/while/body/eval_jaxpr/ppermute | solution.py:17
  186.3 15.0 %collective-permute-start.1 = (f32[8,8,32,1]{2,1,3,0:T(8,128)S(1)}, f32[8,8,32,1]{2,1,3,0:T(8,128)}, u32[]{:S(2)}, u32[]{:S(2)}) collective-permute-start(f32[8,8,32,1]{2,1,3,0:T(8,128)S(1)} %get-tuple-element.161), channel_id=1, source_target_pairs={{0,1},{1,2},{2,3},{3,4},{4,5},{5,6},{6,7},{7,8},{8,9},{9,10},{10,1... | collective-permute-start | bytes 24584 | tf_op jit(solution)/shard_map/while/body/eval_jaxpr/ppermute | solution.py:16
  207.9 16.5 %collective-permute-start = (f32[8,8,32,1]{2,1,3,0:T(8,128)S(1)}, f32[8,8,32,1]{2,1,3,0:T(8,128)S(1)}, u32[]{:S(2)}, u32[]{:S(2)}) collective-permute-start(f32[8,8,32,1]{2,1,3,0:T(8,128)S(1)} %get-tuple-element.160), channel_id=1, source_target_pairs={{1,0},{2,1},{3,2},{4,3},{5,4},{6,5},{7,6},{8,7},{9,8},{10,9},{11,1... | collective-permute-start | bytes 24584 | tf_op jit(solution)/shard_map/while/body/eval_jaxpr/ppermute | solution.py:17
  209.9 15.0 %collective-permute-start.1 = (f32[8,8,32,1]{2,1,3,0:T(8,128)S(1)}, f32[8,8,32,1]{2,1,3,0:T(8,128)}, u32[]{:S(2)}, u32[]{:S(2)}) collective-permute-start(f32[8,8,32,1]{2,1,3,0:T(8,128)S(1)} %get-tuple-element.161), channel_id=1, source_target_pairs={{0,1},{1,2},{2,3},{3,4},{4,5},{5,6},{6,7},{7,8},{8,9},{9,10},{10,1... | collective-permute-start | bytes 24584 | tf_op jit(solution)/shard_map/while/body/eval_jaxpr/ppermute | solution.py:16
  231.5 16.5 %collective-permute-start = (f32[8,8,32,1]{2,1,3,0:T(8,128)S(1)}, f32[8,8,32,1]{2,1,3,0:T(8,128)S(1)}, u32[]{:S(2)}, u32[]{:S(2)}) collective-permute-start(f32[8,8,32,1]{2,1,3,0:T(8,128)S(1)} %get-tuple-element.160), channel_id=1, source_target_pairs={{1,0},{2,1},{3,2},{4,3},{5,4},{6,5},{7,6},{8,7},{9,8},{10,9},{11,1... | collective-permute-start | bytes 24584 | tf_op jit(solution)/shard_map/while/body/eval_jaxpr/ppermute | solution.py:17
  233.4 15.0 %collective-permute-start.1 = (f32[8,8,32,1]{2,1,3,0:T(8,128)S(1)}, f32[8,8,32,1]{2,1,3,0:T(8,128)}, u32[]{:S(2)}, u32[]{:S(2)}) collective-permute-start(f32[8,8,32,1]{2,1,3,0:T(8,128)S(1)} %get-tuple-element.161), channel_id=1, source_target_pairs={{0,1},{1,2},{2,3},{3,4},{4,5},{5,6},{6,7},{7,8},{8,9},{9,10},{10,1... | collective-permute-start | bytes 24584 | tf_op jit(solution)/shard_map/while/body/eval_jaxpr/ppermute | solution.py:16
  255.0 16.5 %collective-permute-start = (f32[8,8,32,1]{2,1,3,0:T(8,128)S(1)}, f32[8,8,32,1]{2,1,3,0:T(8,128)S(1)}, u32[]{:S(2)}, u32[]{:S(2)}) collective-permute-start(f32[8,8,32,1]{2,1,3,0:T(8,128)S(1)} %get-tuple-element.160), channel_id=1, source_target_pairs={{1,0},{2,1},{3,2},{4,3},{5,4},{6,5},{7,6},{8,7},{9,8},{10,9},{11,1... | collective-permute-start | bytes 24584 | tf_op jit(solution)/shard_map/while/body/eval_jaxpr/ppermute | solution.py:17
  256.9 15.0 %collective-permute-start.1 = (f32[8,8,32,1]{2,1,3,0:T(8,128)S(1)}, f32[8,8,32,1]{2,1,3,0:T(8,128)}, u32[]{:S(2)}, u32[]{:S(2)}) collective-permute-start(f32[8,8,32,1]{2,1,3,0:T(8,128)S(1)} %get-tuple-element.161), channel_id=1, source_target_pairs={{0,1},{1,2},{2,3},{3,4},{4,5},{5,6},{6,7},{7,8},{8,9},{9,10},{10,1... | collective-permute-start | bytes 24584 | tf_op jit(solution)/shard_map/while/body/eval_jaxpr/ppermute | solution.py:16
  278.6 16.5 %collective-permute-start = (f32[8,8,32,1]{2,1,3,0:T(8,128)S(1)}, f32[8,8,32,1]{2,1,3,0:T(8,128)S(1)}, u32[]{:S(2)}, u32[]{:S(2)}) collective-permute-start(f32[8,8,32,1]{2,1,3,0:T(8,128)S(1)} %get-tuple-element.160), channel_id=1, source_target_pairs={{1,0},{2,1},{3,2},{4,3},{5,4},{6,5},{7,6},{8,7},{9,8},{10,9},{11,1... | collective-permute-start | bytes 24584 | tf_op jit(solution)/shard_map/while/body/eval_jaxpr/ppermute | solution.py:17
  280.5 15.0 %collective-permute-start.1 = (f32[8,8,32,1]{2,1,3,0:T(8,128)S(1)}, f32[8,8,32,1]{2,1,3,0:T(8,128)}, u32[]{:S(2)}, u32[]{:S(2)}) collective-permute-start(f32[8,8,32,1]{2,1,3,0:T(8,128)S(1)} %get-tuple-element.161), channel_id=1, source_target_pairs={{0,1},{1,2},{2,3},{3,4},{4,5},{5,6},{6,7},{7,8},{8,9},{9,10},{10,1... | collective-permute-start | bytes 24584 | tf_op jit(solution)/shard_map/while/body/eval_jaxpr/ppermute | solution.py:16
  302.1 16.5 %collective-permute-start = (f32[8,8,32,1]{2,1,3,0:T(8,128)S(1)}, f32[8,8,32,1]{2,1,3,0:T(8,128)S(1)}, u32[]{:S(2)}, u32[]{:S(2)}) collective-permute-start(f32[8,8,32,1]{2,1,3,0:T(8,128)S(1)} %get-tuple-element.160), channel_id=1, source_target_pairs={{1,0},{2,1},{3,2},{4,3},{5,4},{6,5},{7,6},{8,7},{9,8},{10,9},{11,1... | collective-permute-start | bytes 24584 | tf_op jit(solution)/shard_map/while/body/eval_jaxpr/ppermute | solution.py:17
  304.0 15.0 %collective-permute-start.1 = (f32[8,8,32,1]{2,1,3,0:T(8,128)S(1)}, f32[8,8,32,1]{2,1,3,0:T(8,128)}, u32[]{:S(2)}, u32[]{:S(2)}) collective-permute-start(f32[8,8,32,1]{2,1,3,0:T(8,128)S(1)} %get-tuple-element.161), channel_id=1, source_target_pairs={{0,1},{1,2},{2,3},{3,4},{4,5},{5,6},{6,7},{7,8},{8,9},{9,10},{10,1... | collective-permute-start | bytes 24584 | tf_op jit(solution)/shard_map/while/body/eval_jaxpr/ppermute | solution.py:16
  325.7 16.5 %collective-permute-start = (f32[8,8,32,1]{2,1,3,0:T(8,128)S(1)}, f32[8,8,32,1]{2,1,3,0:T(8,128)S(1)}, u32[]{:S(2)}, u32[]{:S(2)}) collective-permute-start(f32[8,8,32,1]{2,1,3,0:T(8,128)S(1)} %get-tuple-element.160), channel_id=1, source_target_pairs={{1,0},{2,1},{3,2},{4,3},{5,4},{6,5},{7,6},{8,7},{9,8},{10,9},{11,1... | collective-permute-start | bytes 24584 | tf_op jit(solution)/shard_map/while/body/eval_jaxpr/ppermute | solution.py:17
  327.6 15.0 %collective-permute-start.1 = (f32[8,8,32,1]{2,1,3,0:T(8,128)S(1)}, f32[8,8,32,1]{2,1,3,0:T(8,128)}, u32[]{:S(2)}, u32[]{:S(2)}) collective-permute-start(f32[8,8,32,1]{2,1,3,0:T(8,128)S(1)} %get-tuple-element.161), channel_id=1, source_target_pairs={{0,1},{1,2},{2,3},{3,4},{4,5},{5,6},{6,7},{7,8},{8,9},{9,10},{10,1... | collective-permute-start | bytes 24584 | tf_op jit(solution)/shard_map/while/body/eval_jaxpr/ppermute | solution.py:16
  349.2 16.5 %collective-permute-start = (f32[8,8,32,1]{2,1,3,0:T(8,128)S(1)}, f32[8,8,32,1]{2,1,3,0:T(8,128)S(1)}, u32[]{:S(2)}, u32[]{:S(2)}) collective-permute-start(f32[8,8,32,1]{2,1,3,0:T(8,128)S(1)} %get-tuple-element.160), channel_id=1, source_target_pairs={{1,0},{2,1},{3,2},{4,3},{5,4},{6,5},{7,6},{8,7},{9,8},{10,9},{11,1... | collective-permute-start | bytes 24584 | tf_op jit(solution)/shard_map/while/body/eval_jaxpr/ppermute | solution.py:17
  351.1 15.0 %collective-permute-start.1 = (f32[8,8,32,1]{2,1,3,0:T(8,128)S(1)}, f32[8,8,32,1]{2,1,3,0:T(8,128)}, u32[]{:S(2)}, u32[]{:S(2)}) collective-permute-start(f32[8,8,32,1]{2,1,3,0:T(8,128)S(1)} %get-tuple-element.161), channel_id=1, source_target_pairs={{0,1},{1,2},{2,3},{3,4},{4,5},{5,6},{6,7},{7,8},{8,9},{9,10},{10,1... | collective-permute-start | bytes 24584 | tf_op jit(solution)/shard_map/while/body/eval_jaxpr/ppermute | solution.py:16
  (33 other events, 240.8 us)
Sparse Core Ops, SparseCore 0:
  10.5 92.6 all-gather.1
  399.2 340.3 all-reduce.5
where the time goes:
time: 753 us; the launch traced here: 748 us
  waiting for transfers between devices  393 us (52%)
  local copies, waits for them, and re-layouts  185 us (25%)
  starting transfers between devices  85.6 us (11%)
  other arithmetic  70.2 us (9%)
  between operations  13.7 us (2%)
    psum x1, waiting for transfers between devices, body(): summed = lax.psum(stored_terms, 'member')  341 us
    another operation x40, local copies, waits for them, and re-layouts  80.1 us
    ppermute x11, starting transfers between devices, extended_2(): before = lax.ppermute(last, axis, up)  63.7 us
    all_gather x1, waiting for transfers between devices, body(): gathered = lax.all_gather(gradient_store, 'member', axis=3, tiled=True)  51.2 us
    unnamed x24, local copies, waits for them, and re-layouts  29.7 us
    add x11, other arithmetic, diffuse(): coefficient[..., :-2] + coefficient[..., 2:] + neighbours(coeff_mid)  22.9 us
    ppermute x11, starting transfers between devices, extended_2(): after = lax.ppermute(initial, axis, down)  21.8 us
    mul x11, local copies, waits for them, and re-layouts, body(): perturbations[:, slot, var_index].astype(jnp.float32)  16.7 us
  transfers between devices with their start and end apart: 24, of which 2 were waited for; matrix products, arithmetic and copies ran while one was open for 17% of the time, Pallas kernels for 0%

commit v1 on v0

v1 whole, which is shorter than its diff:
```python
import functools

import jax
import jax.numpy as jnp
from jax import lax
from jax.experimental import pallas as pl
from jax.experimental.pallas import tpu as pltpu
from jax.sharding import PartitionSpec as P

MESH = pl.DeviceIdType.MESH
F32 = jnp.float32
SWEEPS = 10
SV = 10
M = 8
NZ = 8
NY = 32
RING = 8
ROW = NZ * M
VMEM = pl.BlockSpec(memory_space=pltpu.VMEM)
SMEM = pl.BlockSpec(memory_space=pltpu.SMEM)
LIMIT = 60 * 1024 * 1024


def lanes(rows):
    return lax.broadcasted_iota(jnp.int32, (rows, 128), 1)


def roll(value, shift):
    shift = shift % 128
    return value if shift == 0 else pltpu.roll(value, shift, 1)


def up(row, above):
    cut = row.shape[0] - M
    return jnp.concatenate([row[:cut] + above[M:], row[cut:]], axis=0)


def six(p0, pu, cur, nxt):
    u = up(nxt, cur)
    four = u + jnp.concatenate([p0, pu[: ROW - M]], axis=0)
    return four + (roll(cur, 1) + roll(cur, 127)), u


def main_pass(src, emit, unroll=2):
    cur = src[pl.ds(0, ROW), :]

    def body(y, carry):
        p0, pu, cur = carry
        nxt = src[pl.ds(pl.multiple_of((y + 1) * ROW, ROW), ROW), :]
        total, u = six(p0, pu, cur, nxt)
        emit(pl.ds(pl.multiple_of(y * ROW, ROW), ROW), cur, total)
        return cur[:M], u, nxt

    lax.fori_loop(0, NY, body, (jnp.zeros((M, 128), F32), cur, cur), unroll=unroll)


def strip_pass(src, lo, hi, emit):
    first, last = src[pl.ds(0, ROW), :], src[pl.ds(7 * ROW, ROW), :]
    prev = jnp.where(lo, 0.0, roll(last, 32))
    beyond = jnp.where(hi, 0.0, roll(first, 96))
    p0, pu, cur = prev[:M], up(first, prev), first
    for y in range(8):
        nxt = src[pl.ds((y + 1) * ROW, ROW), :] if y < 7 else beyond
        total, u = six(p0, pu, cur, nxt)
        emit(pl.ds(y * ROW, ROW), cur, total)
        p0, pu, cur = cur[:M], u, nxt


def strip_masks():
    lane = lanes(ROW)
    left = ((lane >= 118) | (lane < 22), (lane >= 86) & (lane < 118))
    right = ((lane >= 106) | (lane < 10), (lane >= 74) & (lane < 106))
    return left, right


def coefficients(src, dst_a, dst_q, strip=None):
    def emit(rows, cur, total):
        dst_a[rows, :] = 1.0 - cur * total
        dst_q[rows, :] = cur * cur

    if strip is None:
        main_pass(src, emit)
    else:
        strip_pass(src, *strip, emit)


def stepper(dst, a, q):
    def emit(rows, cur, total):
        dst[rows, :] = a[rows, :] * cur + q[rows, :] * total

    return emit


def k_strips(k_ref, left_ref, right_ref):
    region = lanes(8) // 32
    for z in range(NZ):
        turned = [roll(k_ref[z, pl.ds(8 * h, 8), :], 32 * h) for h in range(4)]
        left, right = turned[0], turned[0]
        for h in range(1, 4):
            left = jnp.where(region == h, turned[h], left)
            right = jnp.where(region == h - 1, turned[h], right)
        left_ref[z] = left
        right_ref[z] = right


def spread(value_of, dst, blocks, pad=True):
    def body(z, carry):
        for b in range(blocks):
            value = value_of(z, b)
            for m in range(M):
                dst[pl.ds(b * 8 * ROW + z * M + m, 8, stride=ROW), :] = value
        return carry

    lax.fori_loop(0, NZ, body, 0)


def prepare_kernel(k_ref, kl_ref, kr_ref, a_ref, q_ref, kb):
    k_strips(k_ref, kl_ref, kr_ref)
    kb[pl.ds(NY * ROW, ROW), :] = jnp.zeros((ROW, 128), F32)
    spread(lambda z, b: k_ref[z, pl.ds(8 * b, 8), :], kb, 4)
    coefficients(kb, a_ref, q_ref)


def strip_prepare(kl_ref, kr_ref, hl_ref, hr_ref, al, ql, ar, qr, kb):
    lane = lanes(8) % 32
    left, right = strip_masks()
    spread(lambda z, b: jnp.where(lane >= 22, hl_ref[z], kl_ref[z]), kb, 1)
    coefficients(kb, al, ql, left)
    spread(lambda z, b: jnp.where(lane < 10, hr_ref[z], kr_ref[z]), kb, 1)
    coefficients(kb, ar, qr, right)


def member(zh, y, c):
    return {"member": (zh * RING + lax.rem(y + RING, RING)) * 2 + c}


def here():
    i = lax.axis_index("member")
    return i // (2 * RING), lax.rem(i // 2, RING), lax.rem(i, 2)


def greet(targets, conditional=()):
    barrier = pltpu.get_barrier_semaphore()
    count = len(targets)
    for target in targets:
        pl.semaphore_signal(barrier, inc=1, device_id=target, device_id_type=MESH)
    for condition, target in conditional:
        @pl.when(condition)
        def _():
            pl.semaphore_signal(barrier, inc=1, device_id=target, device_id_type=MESH)

        count = count + jnp.where(condition, 1, 0)
    pl.semaphore_wait(barrier, count)


def copy_to(src, dst, send, recv, target):
    return pltpu.make_async_remote_copy(
        src_ref=src, dst_ref=dst, send_sem=send, recv_sem=recv, device_id=target, device_id_type=MESH
    )


def tile_links():
    t, n = lax.axis_index("tile"), lax.axis_size("tile")
    return (t > 0, {"tile": lax.rem(t + n - 1, n)}), (t < n - 1, {"tile": lax.rem(t + 1, n)})


def halo_start(to_left, to_right, from_left, from_right, send, recv):
    (has_left, left), (has_right, right) = tile_links()
    rightward = copy_to(to_right, from_left, send.at[0], recv.at[0], right)
    leftward = copy_to(to_left, from_right, send.at[1], recv.at[1], left)

    @pl.when(has_right)
    def _():
        rightward.start()

    @pl.when(has_left)
    def _():
        leftward.start()

    @pl.when(jnp.logical_not(has_left))
    def _():
        from_left[...] = jnp.zeros(from_left.shape, F32)

    @pl.when(jnp.logical_not(has_right))
    def _():
        from_right[...] = jnp.zeros(from_right.shape, F32)

    def finish():
        @pl.when(has_right)
        def _():
            rightward.wait_send()
            leftward.wait_recv()

        @pl.when(has_left)
        def _():
            leftward.wait_send()
            rightward.wait_recv()

    return finish


def gather_kernel(grad, kl, kr, full, hl, hr, y_send, y_recv, p_send, p_recv, z_sem, local_sem, h_send, h_recv):
    zh, y, c = here()
    near = [member(zh, y + d, c) for d in (1, 2, -1, -2)]
    anti, pair = member(1 - zh, y, c), member(zh, y, 1 - c)
    greet(near + [anti, pair], tile_links())

    half = SV * NZ // 2
    lower, upper = pl.ds(0, half), pl.ds(half, half)
    waits = []

    def slot(side, d, core=c):
        z = zh if side == 0 else 1 - zh
        return member(z, y + d, core)["member"]

    mine = pltpu.make_async_copy(grad, full.at[slot(0, 0)], local_sem)
    mine.start()

    def y_copy(side, kind, source_block=None):
        d, to, rows = {
            0: (0, 1, None), 1: (0, 2, None), 2: (0, -1, None), 3: (0, -2, None),
            4: (-2, 1, None), 5: (-2, 2, lower), 6: (2, -1, None), 7: (2, -2, upper),
        }[kind]
        place = full.at[slot(side, d)] if rows is None else full.at[slot(side, d), rows]
        source = place if source_block is None else source_block
        return copy_to(source, place, y_send.at[side, kind], y_recv.at[side, kind], near[{1: 0, 2: 1, -1: 2, -2: 3}[to]])

    def y_start(side, kind, source_block=None):
        op = y_copy(side, kind, source_block)
        op.start()
        waits.append(op)

    def y_arrived(side, kind):
        y_copy(side, kind).wait_recv()

    def pass_on(number, place, source=None):
        op = copy_to(place if source is None else source, place, p_send.at[number], p_recv.at[number], pair)
        op.start()
        waits.append(op)

    cross = copy_to(grad, full.at[slot(0, 0)], z_sem.at[0], z_sem.at[1], anti)
    cross.start()
    for kind in (1, 3, 0, 2):
        y_start(0, kind, grad)
    pass_on(0, full.at[slot(0, 0)], grad)
    halos = halo_start(kl, kr, hl, hr, h_send, h_recv)

    def arrivals(side, kinds):
        for kind in kinds:
            y_arrived(side, kind)
            d, rows = {
                0: (-1, None), 1: (-2, None), 2: (1, None), 3: (2, None),
                4: (-3, None), 5: (-4, lower), 6: (3, None), 7: (4, upper),
            }[kind]
            if kind == 1:
                y_start(side, 5)
                y_start(side, 4)
            if kind == 3:
                y_start(side, 7)
                y_start(side, 6)
            place = full.at[slot(side, d)] if rows is None else full.at[slot(side, d), rows]
            pass_on(1 + side * 9 + kind, place)

    arrivals(0, (0, 2, 1, 3))
    cross.wait_recv()
    for kind in (1, 3, 0, 2):
        y_start(1, kind)
    pass_on(9, full.at[slot(1, 0)])
    arrivals(0, (4, 6, 5, 7))
    arrivals(1, (0, 2, 1, 3, 4, 6, 5, 7))

    halos()
    mine.wait()
    cross.wait_send()
    for op in waits:
        op.wait_send()
    for number in range(18):
        side, kind = divmod(number - 1, 9) if number else (0, None)
        if number in (0, 9):
            place = full.at[slot(0 if number == 0 else 1, 0, 1 - c)]
        else:
            d, rows = {
                0: (-1, None), 1: (-2, None), 2: (1, None), 3: (2, None),
                4: (-3, None), 5: (-4, lower), 6: (3, None), 7: (4, upper),
            }[kind]
            place = full.at[slot(side, d, 1 - c)]
            place = place if rows is None else place.at[rows]
        copy_to(place, place, p_send.at[number], p_recv.at[number], pair).wait_recv()


def weigh_kernel(owner, full, pert, k_ref, state, pad_rows, gt):
    state[pl.ds(NY * ROW, ROW), :] = jnp.zeros((ROW, 128), F32)

    def regroup(y, carry):
        o = owner[y]
        for sv in range(SV):
            gt[pl.ds(sv * NZ * NY + y, NZ, stride=NY), :] = full[o, pl.ds(sv * NZ, NZ), :]
        return carry

    lax.fori_loop(0, NY, regroup, 0)

    def body(i, carry):
        z, b = i // 2, lax.rem(i, 2)
        y0 = pl.multiple_of(b * 16, 16)
        grads = [gt[pl.ds(pl.multiple_of(sv * NZ * NY + z * NY + y0, 16), 16), :] for sv in range(SV)]
        k = k_ref[z, pl.ds(y0, 16), :]
        for m in range(M):
            total = None
            for sv in range(SV):
                term = pert[m, sv, z, pl.ds(y0, 16), :].astype(F32) * grads[sv]
                total = term if total is None else total + term
            total = total * k
            for part in range(2):
                start = (y0 + 8 * part) * ROW + z * M + m
                state[pl.ds(start, 8, stride=ROW), :] = total[8 * part : 8 * part + 8]
        return carry

    lax.fori_loop(0, 2 * NZ, body, 0)


def cut_strips(state, vl, vr):
    region = lanes(ROW) // 32

    def body(y, carry):
        turned = [roll(state[pl.ds(pl.multiple_of((8 * h + y) * ROW, ROW), ROW), :], 32 * h) for h in range(4)]
        left, right = turned[0], turned[0]
        for h in range(1, 4):
            left = jnp.where(region == h, turned[h], left)
            right = jnp.where(region == h - 1, turned[h], right)
        rows = pl.ds(pl.multiple_of(y * ROW, ROW), ROW)
        vl[rows, :] = left
        vr[rows, :] = right
        return carry

    lax.fori_loop(0, 8, body, 0)


def evens(row, odd):
    return jnp.concatenate([row[M * (2 * i + odd) : M * (2 * i + odd + 1)] for i in range(4)], axis=0)


def pack_strips(vl, vr, to_left, to_right):
    lane = lanes(ROW // 2) % 32

    def body(y, carry):
        rows = pl.ds(pl.multiple_of(y * ROW, ROW), ROW)
        out = pl.ds(pl.multiple_of(y * ROW // 2, ROW // 2), ROW // 2)
        right, left = vr[rows, :], vl[rows, :]
        to_right[out, :] = jnp.where(lane >= 22, evens(right, 0), roll(evens(right, 1), 118))
        to_left[out, :] = jnp.where(lane < 10, evens(left, 0), roll(evens(left, 1), 10))
        return carry

    lax.fori_loop(0, 8, body, 0)


def unpack_strips(from_left, from_right, vl, vr):
    lane = lanes(ROW) % 32

    def mixed(even, odd):
        return jnp.concatenate([part[M * i : M * i + M] for i in range(4) for part in (even, odd)], axis=0)

    def body(y, carry):
        rows = pl.ds(pl.multiple_of(y * ROW, ROW), ROW)
        packed = pl.ds(pl.multiple_of(y * ROW // 2, ROW // 2), ROW // 2)
        left, right = from_left[packed, :], from_right[packed, :]
        vl[rows, :] = jnp.where(lane >= 22, mixed(left, roll(left, 10)), vl[rows, :])
        vr[rows, :] = jnp.where(lane < 10, mixed(right, roll(right, 118)), vr[rows, :])
        return carry

    lax.fori_loop(0, 8, body, 0)


def halo_kernel(to_left, to_right, from_left, from_right, send, recv):
    greet([], tile_links())
    halo_start(to_left, to_right, from_left, from_right, send, recv)()


def cut_kernel(state, vl, vr, to_left, to_right):
    cut_strips(state, vl, vr)
    pack_strips(vl, vr, to_left, to_right)


def merge_strips(state, vl, vr):
    lane = lanes(ROW)
    inner = (lane >= 10) & (lane < 118)

    def body(y, carry):
        rows = pl.ds(pl.multiple_of(y * ROW, ROW), ROW)
        edge = jnp.where(lane % 32 < 10, vl[rows, :], vr[rows, :])
        for h in range(4):
            place = pl.ds(pl.multiple_of((8 * h + y) * ROW, ROW), ROW)
            state[place, :] = jnp.where(inner, state[place, :], roll(edge, -32 * h))
        return carry

    lax.fori_loop(0, 8, body, 0)


def second_pass(pert, k_ref, state, inc, norm):
    def body(i, carry):
        z, b = i // 2, lax.rem(i, 2)
        y0 = pl.multiple_of(b * 16, 16)
        factor = norm / k_ref[z, pl.ds(y0, 16), :]
        local = []
        for m in range(M):
            starts = [(y0 + 8 * part) * ROW + z * M + m for part in range(2)]
            local.append(jnp.concatenate([state[pl.ds(s, 8, stride=ROW), :] for s in starts], axis=0))
        for sv in range(SV):
            total = None
            for m in range(M):
                term = pert[m, sv, z, pl.ds(y0, 16), :].astype(F32) * local[m]
                total = term if total is None else total + term
            total = total * factor
            for part in range(2):
                start = (y0 + 8 * part) * SV * NZ + sv * NZ + z
                inc[pl.ds(start, 8, stride=SV * NZ), :] = total[8 * part : 8 * part + 8]
        return carry

    lax.fori_loop(0, 2 * NZ, body, 0)


def sweep_kernel(slab_of, pert, k_ref, a, q, kl, kr, hl, hr, state0, vl0, vr0, from_left, from_right, out,
                 s0, s1, l0, l1, r0, r1, al, ql, ar, qr, kb, inc, *, norm):
    strip_prepare(kl, kr, hl, hr, al, ql, ar, qr, kb)
    left, right = strip_masks()
    s0[...] = state0[...]
    l0[...] = vl0[...]
    r0[...] = vr0[...]
    s1[pl.ds(NY * ROW, ROW), :] = jnp.zeros((ROW, 128), F32)
    unpack_strips(from_left, from_right, l0, r0)

    def two(i, carry):
        main_pass(s0, stepper(s1, a, q))
        main_pass(s1, stepper(s0, a, q))
        strip_pass(l0, *left, stepper(l1, al, ql))
        strip_pass(r0, *right, stepper(r1, ar, qr))
        strip_pass(l1, *left, stepper(l0, al, ql))
        strip_pass(r1, *right, stepper(r0, ar, qr))
        return carry

    lax.fori_loop(0, SWEEPS // 2, two, 0)
    merge_strips(s0, l0, r0)
    second_pass(pert, k_ref, s0, inc, norm)
    core = lax.rem(lax.axis_index("member"), 2)

    def order(d, carry):
        for other in range(2):
            row = slab_of[2 * d + (core if other == 0 else 1 - core)]
            out[other, d] = inc[pl.ds(pl.multiple_of(row * SV * NZ, SV * NZ), SV * NZ), :]
        return carry

    lax.fori_loop(0, 2 * RING, order, 0)


def reduce_kernel(sums, out, total, other, step_buf, z_buf, p_send, p_recv, y_send, y_recv, z_sem):
    zh, y, c = here()
    up_to, down_to = member(zh, y + 1, c), member(zh, y - 1, c)
    anti, pair = member(1 - zh, y, c), member(zh, y, 1 - c)
    greet([up_to, down_to, anti, pair])
    half = SV * NZ // 2
    lower, upper = pl.ds(0, half), pl.ds(half, half)
    waits = []

    def block(side, d):
        return (zh if side == 0 else 1 - zh) * RING + lax.rem(y + d + RING, RING)

    order = (4, 3, -3, 2, -2, 1, -1, 0)
    pair_ops = {}
    for n, d in enumerate(order):
        for side in (1, 0):
            b = block(side, d)
            op = copy_to(sums.at[1, b], other.at[b], p_send.at[side, n], p_recv.at[side, n], pair)
            op.start()
            waits.append(op)
            pair_ops[side, d] = op

    def paired(d):
        for side in (1, 0):
            pair_ops[side, d].wait_recv()
            b = block(side, d)
            total[b] = sums[0, b] + other[b]

    def ring(side, direction, k):
        b = block(side, direction * (5 - k))
        rows = (lower if direction > 0 else upper) if k == 1 else pl.ds(0, SV * NZ)
        way = 0 if direction > 0 else 1
        return copy_to(
            total.at[b, rows], step_buf.at[side, way, k - 1, rows], y_send.at[side, way, k - 1],
            y_recv.at[side, way, k - 1], up_to if direction > 0 else down_to,
        )

    paired(4)
    for side in (1, 0):
        for direction in (1, -1):
            op = ring(side, direction, 1)
            op.start()
            waits.append(op)
    for k in (2, 3, 4, 5):
        paired(5 - k)
        if k < 5:
            paired(k - 5)
        for side in (1, 0):
            for direction in (1, -1):
                way = 0 if direction > 0 else 1
                ring(side, direction, k - 1).wait_recv()
                b = block(side, direction * (5 - k))
                if k == 2:
                    rows = lower if direction > 0 else upper
                    total[b, rows, :] += step_buf[side, way, 0, rows, :]
                else:
                    total[b] += step_buf[side, way, k - 2]
                if k < 5:
                    op = ring(side, direction, k)
                    op.start()
                    waits.append(op)
            if k == 5 and side == 1:
                cross = copy_to(total.at[block(1, 0)], z_buf, z_sem.at[0], z_sem.at[1], anti)
                cross.start()
    cross.wait()
    out[...] = total[block(0, 0)] + z_buf[...]
    for op in waits:
        op.wait_send()


def params(collective=None):
    if collective is None:
        return pltpu.CompilerParams(vmem_limit_bytes=LIMIT)
    return pltpu.CompilerParams(vmem_limit_bytes=LIMIT, collective_id=collective, has_side_effects=True)


def f32(*shape):
    return jax.ShapeDtypeStruct(shape, F32)


def call(kernel, outs, ins, scratch=(), collective=None):
    return pl.pallas_call(
        kernel,
        out_shape=outs,
        in_specs=ins,
        out_specs=[VMEM] * len(outs),
        scratch_shapes=list(scratch),
        compiler_params=params(collective),
    )


def body(perturbations, gradient_store, diffusivity, slab_owner):
    members = perturbations.shape[0] * lax.axis_size("member")
    pert = perturbations.reshape(M, SV, NZ, NY, 128)
    grad = gradient_store.reshape(SV * NZ, 128)
    own = jnp.arange(NY, dtype=jnp.int32)
    slab_of = jnp.sum(jnp.where(slab_owner[None, :] == own[:, None], own[None, :], 0), axis=1)
    dma, scr = pltpu.SemaphoreType.DMA, pltpu.VMEM
    big, strip = (NY * ROW, 128), (8 * ROW, 128)
    state_shape, packed = ((NY + 1) * ROW, 128), (4 * ROW, 128)

    kl, kr, a, q = call(
        prepare_kernel, [f32(NZ, 8, 128)] * 2 + [f32(*big)] * 2, [VMEM], [scr(state_shape, F32)]
    )(diffusivity)
    full, hl, hr = call(
        gather_kernel, [f32(2 * 2 * RING, SV * NZ, 128), f32(NZ, 8, 128), f32(NZ, 8, 128)], [VMEM] * 3,
        [dma((2, 8)), dma((2, 8)), dma((19,)), dma((19,)), dma((2,)), dma, dma((2,)), dma((2,))], 0,
    )(grad, kl, kr)
    state, unused = call(
        weigh_kernel, [f32(*state_shape), f32(8, 128)], [SMEM, VMEM, VMEM, VMEM], [scr((SV * NZ * NY, 128), F32)]
    )(slab_owner, full, pert, diffusivity)
    vl, vr, to_left, to_right = call(cut_kernel, [f32(*strip)] * 2 + [f32(*packed)] * 2, [VMEM])(state)
    from_left, from_right = call(halo_kernel, [f32(*packed)] * 2, [VMEM] * 2, [dma((2,)), dma((2,))], 1)(to_left, to_right)
    (sums,) = call(
        functools.partial(sweep_kernel, norm=1.0 / (members - 1)),
        [f32(2, 2 * RING, SV * NZ, 128)],
        [SMEM] + [VMEM] * 13,
        [scr(state_shape, F32)] * 2 + [scr(strip, F32)] * 9 + [scr((NY * SV * NZ, 128), F32)],
    )(slab_of, pert, diffusivity, a, q, kl, kr, hl, hr, state, vl, vr, from_left, from_right)
    (out,) = call(
        reduce_kernel, [f32(SV * NZ, 128)], [VMEM],
        [scr((2 * RING, SV * NZ, 128), F32)] * 2 + [scr((2, 2, 4, SV * NZ, 128), F32), scr((SV * NZ, 128), F32)]
        + [dma((2, 8)), dma((2, 8)), dma((2, 2, 4)), dma((2, 2, 4)), dma((2,))], 2,
    )(sums)
    return out.reshape(gradient_store.shape)


def solution(mesh):
    in_specs = (
        P("member", None, None, None, None, "tile"),
        P(None, None, None, "member", "tile"),
        P(None, None, "tile"),
        P(),
    )
    out_specs = P(None, None, None, "member", "tile")
    return jax.shard_map(body, mesh=mesh, in_specs=in_specs, out_specs=out_specs, check_vma=False)
```

time: 753 us -> 112 us (0.15)
  waiting for transfers between devices: 393 us -> 0 us
  local copies, waits for them, and re-layouts: 185 us -> 1.4 us
  Pallas kernels: 0 us -> 108 us
  starting transfers between devices: 85.6 us -> 0 us
  other arithmetic: 70.2 us -> 1.35 us
  between operations: 13.7 us -> 0.03 us
    psum x1 -> x0, waiting for transfers between devices: 341 us -> none  [body(): summed = lax.psum(stored_terms, 'member')]
    pallas_call x0 -> x7, Pallas kernels: none -> 108 us  [the longest x1 29.7 us: body(): call(gather_kernel, [f32(2 * 2 * RING, SV * NZ, 128), f32(NZ, 8, 128), f3...]
    ppermute x22 -> x0, starting transfers between devices: 85.5 us -> none  [the longest x11 63.7 us: extended_2(): before = lax.ppermute(last, axis, up)]
    another operation x42 -> x0, local copies, waits for them, and re-layouts: 80.8 us -> none
    all_gather x1 -> x0, waiting for transfers between devices: 51.2 us -> none  [body(): gathered = lax.all_gather(gradient_store, 'member', axis=3, tiled=True)]
    add x22 -> x0, other arithmetic: 41.4 us -> none  [the longest x11 22.9 us: diffuse(): coefficient[..., :-2] + coefficient[..., 2:] + neighbours(coeff_mid)]
    unnamed x24 -> x1, local copies, waits for them, and re-layouts: 29.7 us -> 1.4 us
    slice x22 -> x0, local copies, waits for them, and re-layouts: 18.6 us -> none  [the longest x11 10 us: extended_2(): last = lax.slice_in_dim(array, length - width, length, axis=dim)]
  transfers between devices with their start and end apart: 24 -> 0, of which waited for: 2 -> 0; matrix products, arithmetic and copies ran while one was open for 17% -> 0% of each run, Pallas kernels for 0% -> 0%
where the time goes in v1:
time: 112 us; the launch traced here: 111 us
  Pallas kernels  108 us (96%)
  local copies, waits for them, and re-layouts  1.4 us (1%)
  other arithmetic  1.35 us (1%)
    pallas_call x1, Pallas kernels, body(): call(gather_kernel, [f32(2 * 2 * RING, SV * NZ, 128), f32(NZ, 8, 128), f3...  29.7 us
    pallas_call x1, Pallas kernels, body(): call(functools.partial(sweep_kernel, norm=1.0 / (members - 1)), [f32(2, 2...  29 us
    pallas_call x1, Pallas kernels, body(): call(reduce_kernel, [f32(SV * NZ, 128)], [VMEM], [scr((2 * RING, SV * NZ,...  24.8 us
    pallas_call x1, Pallas kernels, body(): call(halo_kernel, [f32(*packed)] * 2, [VMEM] * 2, [dma((2,)), dma((2,))], 1)  10.3 us
    pallas_call x1, Pallas kernels, body(): call(weigh_kernel, [f32(*state_shape), f32(8, 128)], [SMEM, VMEM, VMEM, V...  6.72 us
    pallas_call x1, Pallas kernels, body(): call(prepare_kernel, [f32(NZ, 8, 128)] * 2 + [f32(*big)] * 2, [VMEM], [sc...  4.5 us
    pallas_call x1, Pallas kernels, body(): call(cut_kernel, [f32(*strip)] * 2 + [f32(*packed)] * 2, [VMEM])(state)  3.43 us

profile of v1, /device:TPU:6, one launch (start us, length us, event | category | flops | bytes accessed | tf_op | source)
XLA Modules:
  0.0 111.2 jit_solution(7063408764541900286)
XLA Ops:
  0.0 1.3 %select_reduce_fusion.slab_of = s32[32]{0:T(128)} fusion(s32[32]{0:T(128)} %owner.1), kind=kLoop, calls=%fused_computation | loop fusion | flops 3040 | bytes 256 | tf_op jit(solution)/shard_map/reduce_sum | solution.py:550
  1.3 4.5 %shard_map.46 = (f32[8,8,128]{2,1,0:T(8,128)}, f32[8,8,128]{2,1,0:T(8,128)}, f32[2048,128]{1,0:T(8,128)}, f32[2048,128]{1,0:T(8,128)}) custom-call(f32[8,32,128]{2,1,0:T(8,128)} %k_ref.5), custom_call_target="tpu_custom_call" | custom-call | tf_op jit(solution)/shard_map/pallas_call | solution.py:555
  5.8 29.7 %shard_map.47 = (f32[32,80,128]{2,1,0:T(8,128)}, f32[8,8,128]{2,1,0:T(8,128)}, f32[8,8,128]{2,1,0:T(8,128)}) custom-call(f32[80,128]{1,0:T(8,128)} %bitcast.8, f32[8,8,128]{2,1,0:T(8,128)} %get-tuple-element.21.kl, f32[8,8,128]{2,1,0:T(8,128)} %get-tuple-element.22.kr), custom_call_target="tpu_custom_call" | custom-call | tf_op jit(solution)/shard_map/pallas_call | solution.py:558
  35.6 6.7 %shard_map.48 = (f32[2112,128]{1,0:T(8,128)}, f32[8,128]{1,0:T(8,128)}) custom-call(s32[32]{0:T(128)} %owner.1, f32[32,80,128]{2,1,0:T(8,128)} %get-tuple-element.25.full, bf16[8,10,8,32,128]{4,3,2,1,0:T(8,128)(2,1)} %bitcast.5, f32[8,32,128]{2,1,0:T(8,128)} %k_ref.5), custom_call_target="tpu_custom_call" | custom-call | tf_op jit(solution)/shard_map/pallas_call | solution.py:562
  42.3 3.4 %shard_map.49 = (f32[512,128]{1,0:T(8,128)}, f32[512,128]{1,0:T(8,128)}, f32[256,128]{1,0:T(8,128)}, f32[256,128]{1,0:T(8,128)}) custom-call(f32[2112,128]{1,0:T(8,128)} %get-tuple-element.26.state.state0), custom_call_target="tpu_custom_call" | custom-call | tf_op jit(solution)/shard_map/pallas_call | solution.py:565
  45.7 10.3 %shard_map.50 = (f32[256,128]{1,0:T(8,128)}, f32[256,128]{1,0:T(8,128)}) custom-call(f32[256,128]{1,0:T(8,128)} %get-tuple-element.29.to_left, f32[256,128]{1,0:T(8,128)} %get-tuple-element.30.to_right), custom_call_target="tpu_custom_call" | custom-call | tf_op jit(solution)/shard_map/pallas_call | solution.py:566
  56.0 29.0 %shard_map.51.sums = f32[2,16,80,128]{3,2,1,0:T(8,128)} custom-call(s32[32]{0:T(128)} %select_reduce_fusion.slab_of, bf16[8,10,8,32,128]{4,3,2,1,0:T(8,128)(2,1)} %bitcast.6, f32[8,32,128]{2,1,0:T(8,128)} %k_ref.5, f32[2048,128]{1,0:T(8,128)} %get-tuple-element.19.a, f32[2048,128]{1,0:T(8,128)} %get-tuple-element.20.q, f32[8,8,128]{2,1,0:T(8,128)} %get-tuple-element.21.kl, ...), custom_call_target="tpu_custom_call" | custom-call | tf_op jit(solution)/shard_map/pallas_call | solution.py:567
  85.0 24.8 %shard_map.52 = f32[80,128]{1,0:T(8,128)} custom-call(f32[2,16,80,128]{3,2,1,0:T(8,128)} %shard_map.51.sums), custom_call_target="tpu_custom_call" | custom-call | tf_op jit(solution)/shard_map/pallas_call | solution.py:573
  109.8 1.4 %copy.8 = f32[2,5,8,1,128]{4,3,2,1,0:T(1,128)} copy(f32[2,5,8,1,128]{4,3,2,1,0:T(1,128)} %bitcast.7) | data formatting | bytes 81920

commit v2 on v1

v2 whole, which is shorter than its diff:
```python
import functools

import jax
import jax.numpy as jnp
from jax import lax
from jax.experimental import pallas as pl
from jax.experimental.pallas import tpu as pltpu
from jax.sharding import PartitionSpec as P

MESH = pl.DeviceIdType.MESH
F32 = jnp.float32
SWEEPS = 10
SV = 10
M = 8
NZ = 8
NY = 32
RING = 8
ROW = NZ * M
VMEM = pl.BlockSpec(memory_space=pltpu.VMEM)
SMEM = pl.BlockSpec(memory_space=pltpu.SMEM)
LIMIT = 60 * 1024 * 1024
UNROLL = 2


def lanes(rows):
    return lax.broadcasted_iota(jnp.int32, (rows, 128), 1)


def roll(value, shift):
    shift = shift % 128
    return value if shift == 0 else pltpu.roll(value, shift, 1)


def up(row, above):
    cut = row.shape[0] - M
    return jnp.concatenate([row[:cut] + above[M:], row[cut:]], axis=0)


def sideways(row):
    return roll(row, 1) + roll(row, 127)


def row_at(y):
    return pl.ds(y * ROW if isinstance(y, int) else pl.multiple_of(y * ROW, ROW), ROW)


def rows_pass(src, count, first, p0, pu, emit, unroll):
    def body(y, carry):
        p0, pu, cur, side = carry
        nxt = src[row_at(y + 1), :]
        beside = sideways(nxt)
        u = up(nxt, cur)
        four = u + jnp.concatenate([p0, pu[: ROW - M]], axis=0)
        emit(row_at(y), cur, four + side)
        return cur[:M], u, nxt, beside

    lax.fori_loop(0, count, body, (p0, pu, first, sideways(first)), unroll=unroll)


def main_pass(src, emit, unroll=UNROLL):
    first = src[row_at(0), :]
    rows_pass(src, NY, first, jnp.zeros((M, 128), F32), first, emit, unroll)


def strip_pass(src, lo, hi, emit, unroll=UNROLL):
    first, last = src[row_at(0), :], src[row_at(7), :]
    prev = jnp.where(lo, 0.0, roll(last, 32))
    src[row_at(8), :] = jnp.where(hi, 0.0, roll(first, 96))
    rows_pass(src, 8, first, prev[:M], up(first, prev), emit, unroll)


def strip_masks():
    lane = lanes(ROW)
    left = ((lane >= 118) | (lane < 22), (lane >= 86) & (lane < 118))
    right = ((lane >= 106) | (lane < 10), (lane >= 74) & (lane < 106))
    return left, right


def coefficients(src, dst_a, dst_q, strip=None):
    def emit(rows, cur, total):
        dst_a[rows, :] = 1.0 - cur * total
        dst_q[rows, :] = cur * cur

    if strip is None:
        main_pass(src, emit)
    else:
        strip_pass(src, *strip, emit)


def stepper(dst, a, q):
    def emit(rows, cur, total):
        dst[rows, :] = a[rows, :] * cur + q[rows, :] * total

    return emit


def k_strips(k_ref, left_ref, right_ref):
    region = lanes(8) // 32
    for z in range(NZ):
        turned = [roll(k_ref[z, pl.ds(8 * h, 8), :], 32 * h) for h in range(4)]
        left, right = turned[0], turned[0]
        for h in range(1, 4):
            left = jnp.where(region == h, turned[h], left)
            right = jnp.where(region == h - 1, turned[h], right)
        left_ref[z] = left
        right_ref[z] = right


def spread(value_of, dst, blocks, pad=True):
    def body(z, carry):
        for b in range(blocks):
            value = value_of(z, b)
            for m in range(M):
                dst[pl.ds(b * 8 * ROW + z * M + m, 8, stride=ROW), :] = value
        return carry

    lax.fori_loop(0, NZ, body, 0)


def strip_prepare(kl_ref, kr_ref, hl_ref, hr_ref, al, ql, ar, qr, kb):
    lane = lanes(8) % 32
    left, right = strip_masks()
    spread(lambda z, b: jnp.where(lane >= 22, hl_ref[z], kl_ref[z]), kb, 1)
    coefficients(kb, al, ql, left)
    spread(lambda z, b: jnp.where(lane < 10, hr_ref[z], kr_ref[z]), kb, 1)
    coefficients(kb, ar, qr, right)


def member(zh, y, c):
    return {"member": (zh * RING + lax.rem(y + RING, RING)) * 2 + c}


def here():
    i = lax.axis_index("member")
    return i // (2 * RING), lax.rem(i // 2, RING), lax.rem(i, 2)


def greet(targets, conditional=()):
    barrier = pltpu.get_barrier_semaphore()
    count = len(targets)
    for target in targets:
        pl.semaphore_signal(barrier, inc=1, device_id=target, device_id_type=MESH)
    for condition, target in conditional:
        @pl.when(condition)
        def _():
            pl.semaphore_signal(barrier, inc=1, device_id=target, device_id_type=MESH)

        count = count + jnp.where(condition, 1, 0)
    pl.semaphore_wait(barrier, count)


def copy_to(src, dst, send, recv, target):
    return pltpu.make_async_remote_copy(
        src_ref=src, dst_ref=dst, send_sem=send, recv_sem=recv, device_id=target, device_id_type=MESH
    )


def tile_links():
    t, n = lax.axis_index("tile"), lax.axis_size("tile")
    return (t > 0, {"tile": lax.rem(t + n - 1, n)}), (t < n - 1, {"tile": lax.rem(t + 1, n)})


def halo_start(to_left, to_right, from_left, from_right, send, recv):
    (has_left, left), (has_right, right) = tile_links()
    rightward = copy_to(to_right, from_left, send.at[0], recv.at[0], right)
    leftward = copy_to(to_left, from_right, send.at[1], recv.at[1], left)

    @pl.when(has_right)
    def _():
        rightward.start()

    @pl.when(has_left)
    def _():
        leftward.start()

    @pl.when(jnp.logical_not(has_left))
    def _():
        from_left[...] = jnp.zeros(from_left.shape, F32)

    @pl.when(jnp.logical_not(has_right))
    def _():
        from_right[...] = jnp.zeros(from_right.shape, F32)

    def finish():
        @pl.when(has_right)
        def _():
            rightward.wait_send()
            leftward.wait_recv()

        @pl.when(has_left)
        def _():
            leftward.wait_send()
            rightward.wait_recv()

    return finish


KINDS = {
    0: (0, 1, 0), 1: (0, 2, 0), 2: (0, -1, 0), 3: (0, -2, 0),
    4: (-2, 1, 0), 5: (-2, 2, 1), 6: (2, -1, 0), 7: (2, -2, 2),
}


def halved(ref, part):
    half = SV * NZ // 2
    return ref if part == 0 else ref.at[pl.ds(0 if part == 1 else half, half)]


def gather(grad, full, near, anti, pair, y_send, y_recv, p_send, p_recv, z_send, z_recv, local_sem, between):
    zh, y, c = here()
    started = []

    def slot(side, d, core):
        return full.at[member(zh if side == 0 else 1 - zh, y + d, core)["member"]]

    def send(op):
        op.start()
        started.append(op)

    def y_copy(side, kind, source=None):
        d, to, part = KINDS[kind]
        place = halved(slot(side, d, c), part)
        return copy_to(place if source is None else source, place, y_send.at[side, kind], y_recv.at[side, kind], near[to])

    def z_copy(kind, source=None):
        d, to, part = KINDS[kind] if kind >= 0 else (0, 0, 0)
        place = halved(slot(0, d - to, c), part)
        n = max(kind - 3, 0)
        return copy_to(place if source is None else source, place, z_send.at[n], z_recv.at[n], anti)

    def p_copy(side, kind, core, source=None):
        d, to, part = KINDS[kind] if kind >= 0 else (0, 0, 0)
        place = halved(slot(side, d - to, core), part)
        n = side * 9 + kind + 1
        return copy_to(place if source is None else source, place, p_send.at[n], p_recv.at[n], pair)

    def arrivals(side, kinds):
        for kind in kinds:
            if side == 1 and kind >= 4:
                z_copy(kind).wait_recv()
            else:
                y_copy(side, kind).wait_recv()
            if side == 0 and kind in (1, 3):
                send(y_copy(0, kind + 4))
                send(y_copy(0, kind + 3))
            if side == 0 and kind >= 4:
                send(z_copy(kind))
            send(p_copy(side, kind, c))

    send(z_copy(-1, grad))
    for kind in (1, 3, 0, 2):
        send(y_copy(0, kind, grad))
    send(p_copy(0, -1, c, grad))
    mine = pltpu.make_async_copy(grad, slot(0, 0, c), local_sem)
    mine.start()
    between[0]()
    arrivals(0, (1, 3, 0, 2))
    z_copy(-1).wait_recv()
    for kind in (1, 3, 0, 2):
        send(y_copy(1, kind))
    send(p_copy(1, -1, c))
    between[1]()
    arrivals(0, (4, 6, 5, 7))
    arrivals(1, (0, 2, 1, 3, 4, 6, 5, 7))
    mine.wait()
    for op in started:
        op.wait_send()
    for side in range(2):
        for kind in range(-1, 8):
            p_copy(side, kind, 1 - c).wait_recv()


def selectors(owner, pick, place):
    lane, row = lanes(8), lax.broadcasted_iota(jnp.int32, (8, 128), 0)
    for y8 in range(0, NY, 8):
        picked = jnp.zeros((8, 128), F32)
        for i in range(8):
            picked = jnp.where((row == i) & (lane % NY == owner[y8 + i]), 1.0, picked)
        pick[pl.ds(y8, 8), :] = picked
    for d8 in range(0, NY, 8):
        placed = jnp.zeros((8, 128), F32)
        for y in range(NY):
            placed = jnp.where((lane % NY == y) & (row + d8 == owner[y]), 1.0, placed)
        place[pl.ds(d8, 8), :] = placed


def permuted(selector, values):
    rhs = jnp.concatenate(values, axis=1)
    high = rhs.astype(jnp.bfloat16)
    low = (rhs - high.astype(F32)).astype(jnp.bfloat16)
    out = jnp.dot(selector, jnp.concatenate([high, low], axis=0), preferred_element_type=F32)
    return out[:, :128], out[:, 128:]


def weigh(pick, full, pert, k_ref, state, gt):
    def regroup(o, carry):
        for sv in range(SV):
            gt[pl.ds(sv * NZ * NY + o, NZ, stride=NY), :] = full[o, pl.ds(sv * NZ, NZ), :]
        return carry

    lax.fori_loop(0, NY, regroup, 0)
    selector = pick[:, pl.ds(0, 2 * NY)].astype(jnp.bfloat16)

    def reorder(z, carry):
        for sv in range(0, SV, 2):
            places = [pl.ds(pl.multiple_of((sv + i) * NZ * NY + z * NY, NY), NY) for i in range(2)]
            for place, value in zip(places, permuted(selector, [gt[place, :] for place in places])):
                gt[place, :] = value
        return carry

    lax.fori_loop(0, NZ, reorder, 0)

    def body(i, carry):
        z, b = i // 2, lax.rem(i, 2)
        y0 = pl.multiple_of(b * 16, 16)
        grads = [gt[pl.ds(pl.multiple_of(sv * NZ * NY + z * NY + y0, 16), 16), :] for sv in range(SV)]
        k = k_ref[z, pl.ds(y0, 16), :]
        for m in range(M):
            total = None
            for sv in range(SV):
                term = pert[m, sv, z, pl.ds(y0, 16), :].astype(F32) * grads[sv]
                total = term if total is None else total + term
            total = total * k
            for part in range(2):
                start = (y0 + 8 * part) * ROW + z * M + m
                state[pl.ds(start, 8, stride=ROW), :] = total[8 * part : 8 * part + 8]
        return carry

    lax.fori_loop(0, 2 * NZ, body, 0)


def cut_strips(state, vl, vr):
    region = lanes(ROW) // 32

    def body(y, carry):
        turned = [roll(state[pl.ds(pl.multiple_of((8 * h + y) * ROW, ROW), ROW), :], 32 * h) for h in range(4)]
        left, right = turned[0], turned[0]
        for h in range(1, 4):
            left = jnp.where(region == h, turned[h], left)
            right = jnp.where(region == h - 1, turned[h], right)
        rows = pl.ds(pl.multiple_of(y * ROW, ROW), ROW)
        vl[rows, :] = left
        vr[rows, :] = right
        return carry

    lax.fori_loop(0, 8, body, 0)


def evens(row, odd):
    return jnp.concatenate([row[M * (2 * i + odd) : M * (2 * i + odd + 1)] for i in range(4)], axis=0)


def pack_strips(vl, vr, to_left, to_right):
    lane = lanes(ROW // 2) % 32

    def body(y, carry):
        rows = pl.ds(pl.multiple_of(y * ROW, ROW), ROW)
        out = pl.ds(pl.multiple_of(y * ROW // 2, ROW // 2), ROW // 2)
        right, left = vr[rows, :], vl[rows, :]
        to_right[out, :] = jnp.where(lane >= 22, evens(right, 0), roll(evens(right, 1), 118))
        to_left[out, :] = jnp.where(lane < 10, evens(left, 0), roll(evens(left, 1), 10))
        return carry

    lax.fori_loop(0, 8, body, 0)


def unpack_strips(from_left, from_right, vl, vr):
    lane = lanes(ROW) % 32

    def mixed(even, odd):
        return jnp.concatenate([part[M * i : M * i + M] for i in range(4) for part in (even, odd)], axis=0)

    def body(y, carry):
        rows = pl.ds(pl.multiple_of(y * ROW, ROW), ROW)
        packed = pl.ds(pl.multiple_of(y * ROW // 2, ROW // 2), ROW // 2)
        left, right = from_left[packed, :], from_right[packed, :]
        vl[rows, :] = jnp.where(lane >= 22, mixed(left, roll(left, 10)), vl[rows, :])
        vr[rows, :] = jnp.where(lane < 10, mixed(right, roll(right, 118)), vr[rows, :])
        return carry

    lax.fori_loop(0, 8, body, 0)


def merge_strips(state, vl, vr):
    lane = lanes(ROW)
    inner = (lane >= 10) & (lane < 118)

    def body(y, carry):
        rows = pl.ds(pl.multiple_of(y * ROW, ROW), ROW)
        edge = jnp.where(lane % 32 < 10, vl[rows, :], vr[rows, :])
        for h in range(4):
            place = pl.ds(pl.multiple_of((8 * h + y) * ROW, ROW), ROW)
            state[place, :] = jnp.where(inner, state[place, :], roll(edge, -32 * h))
        return carry

    lax.fori_loop(0, 8, body, 0)


def second_pass(pert, k_ref, state, natural, inc, place, norm):
    def body(i, carry):
        z, b = i // 2, lax.rem(i, 2)
        y0 = pl.multiple_of(b * 16, 16)
        factor = norm / k_ref[z, pl.ds(y0, 16), :]
        local = []
        for m in range(M):
            starts = [(y0 + 8 * part) * ROW + z * M + m for part in range(2)]
            local.append(jnp.concatenate([state[pl.ds(s, 8, stride=ROW), :] for s in starts], axis=0))
        for sv in range(SV):
            total = None
            for m in range(M):
                term = pert[m, sv, z, pl.ds(y0, 16), :].astype(F32) * local[m]
                total = term if total is None else total + term
            natural[pl.ds(pl.multiple_of(sv * NZ * NY + z * NY + y0, 16), 16), :] = total * factor
        return carry

    lax.fori_loop(0, 2 * NZ, body, 0)
    selector = place[:, pl.ds(0, 2 * NY)].astype(jnp.bfloat16)

    def reorder(z, carry):
        for sv in range(0, SV, 2):
            values = [natural[pl.ds(pl.multiple_of((sv + i) * NZ * NY + z * NY, NY), NY), :] for i in range(2)]
            for i, value in enumerate(permuted(selector, values)):
                for d8 in range(0, NY, 8):
                    inc[pl.ds(d8 * SV * NZ + (sv + i) * NZ + z, 8, stride=SV * NZ), :] = value[d8 : d8 + 8]
        return carry

    lax.fori_loop(0, NZ, reorder, 0)


def reduce(inc, out, total, other, got, near, anti, pair, p_send, p_recv, send_sem, recv_sem):
    zh, y, c = here()
    started = []

    def block(side, d):
        return (zh if side == 0 else 1 - zh) * RING + lax.rem(y + d + RING, RING)

    def p_copy(n):
        b = block(*ORDER[n])
        return copy_to(inc.at[rows_of(b, 1 - c)], other.at[b], p_send.at[n], p_recv.at[n], pair)

    def send(op):
        op.start()
        started.append(op)

    def rows_of(b, core):
        return pl.ds(pl.multiple_of((2 * b + core) * SV * NZ, SV * NZ), SV * NZ)

    def to(n, side, d, target, part=0):
        return copy_to(
            halved(total.at[block(side, d)], part), halved(got.at[n], part), send_sem.at[n], recv_sem.at[n], target
        )

    def paired(side, *ds):
        for d in ds:
            n = ORDER.index((side, d))
            p_copy(n).wait_recv()
            b = block(side, d)
            total[b] = inc[rows_of(b, c), :] + other[b]

    def add(n, side, d, target, part=0):
        to(n, side, d, target, part).wait_recv()
        b = block(side, d)
        if part == 0:
            total[b] += got[n]
        else:
            half = SV * NZ // 2
            rows = pl.ds(0 if part == 1 else half, half)
            total[b, rows, :] += got[n, rows, :]

    for n in range(len(ORDER)):
        send(p_copy(n))

    for n, d in ((0, 4), (1, 3), (2, -3)):
        paired(1, d)
        send(to(n, 1, d, anti))
    for n, d in ((3, 2), (4, -2), (5, 1), (6, -1)):
        paired(1, d)
        send(to(n, 1, d, near[d]))
    paired(0, 4, 3, -3)
    for n, d in ((7, 1), (8, -1)):
        paired(0, d)
        send(to(n, 0, d, near[d]))
    paired(0, 2, -2)
    paired(1, 0)
    paired(0, 0)
    add(0, 0, 4, anti)
    send(to(9, 0, 4, near[2], 1))
    send(to(10, 0, 4, near[-2], 2))
    add(1, 0, 3, anti)
    send(to(11, 0, 3, near[1]))
    add(2, 0, -3, anti)
    send(to(12, 0, -3, near[-1]))
    for n, d in ((5, 1), (6, -1), (3, 2), (4, -2)):
        add(n, 1, 0, near[d])
    send(to(13, 1, 0, anti))
    add(9, 0, 2, near[2], 1)
    add(11, 0, 2, near[1])
    send(to(14, 0, 2, near[2]))
    add(10, 0, -2, near[-2], 2)
    add(12, 0, -2, near[-1])
    send(to(15, 0, -2, near[-2]))
    for n in (7, 8, 13, 14, 15):
        to(n, 0, 0, anti).wait_recv()
    out[...] = ((total[block(0, 0)] + got[7]) + (got[8] + got[13])) + (got[14] + got[15])
    for op in started:
        op.wait_send()


ORDER = (
    (1, 4), (1, 3), (1, -3), (1, 2), (1, -2), (1, 1), (1, -1), (0, 4), (0, 3), (0, -3), (0, 1), (0, -1),
    (0, 2), (0, -2), (1, 0), (0, 0),
)


def kernel(owner, grad, k_ref, pert_in, out, *scratch, norm, names):
    r = dict(zip(names, scratch))
    zh, y, c = here()
    near = {d: member(zh, y + d, c) for d in (1, 2, -1, -2)}
    anti, pair = member(1 - zh, y, c), member(zh, y, 1 - c)
    pert, s0, s1, l0, l1, r0, r1 = (r[n] for n in ("pert", "s0", "s1", "l0", "l1", "r0", "r1"))
    fetch = pltpu.make_async_copy(pert_in, pert, r["pert_sem"])
    fetch.start()
    greet(list(near.values()) + [anti, pair], tile_links())
    left, right = strip_masks()
    kb, halos = r["kb"], []

    def first():
        k_strips(k_ref, r["kl"], r["kr"])
        halos.append(halo_start(r["kl"], r["kr"], r["hl"], r["hr"], r["h_send"], r["h_recv"]))
        kb[row_at(NY), :] = jnp.zeros((ROW, 128), F32)
        s0[row_at(NY), :] = jnp.zeros((ROW, 128), F32)
        s1[row_at(NY), :] = jnp.zeros((ROW, 128), F32)
        spread(lambda z, b: k_ref[z, pl.ds(8 * b, 8), :], kb, 4)
        coefficients(kb, r["a"], r["q"])

    def second():
        selectors(owner, r["pick"], r["place"])
        halos[0]()
        strip_prepare(r["kl"], r["kr"], r["hl"], r["hr"], r["al"], r["ql"], r["ar"], r["qr"], kb)

    gather(
        grad, r["full"], near, anti, pair, r["y_send"], r["y_recv"], r["p_send"], r["p_recv"], r["z_send"], r["z_recv"],
        r["local_sem"], (first, second),
    )
    fetch.wait()
    weigh(r["pick"], r["full"], pert, k_ref, s0, r["gt"])
    cut_strips(s0, l0, r0)
    pack_strips(l0, r0, r["to_left"], r["to_right"])
    finish = halo_start(r["to_left"], r["to_right"], r["from_left"], r["from_right"], r["s_send"], r["s_recv"])

    def two_main(i, carry):
        main_pass(s0, stepper(s1, r["a"], r["q"]))
        main_pass(s1, stepper(s0, r["a"], r["q"]))
        return carry

    def two_strips(i, carry):
        strip_pass(l0, *left, stepper(l1, r["al"], r["ql"]))
        strip_pass(r0, *right, stepper(r1, r["ar"], r["qr"]))
        strip_pass(l1, *left, stepper(l0, r["al"], r["ql"]))
        strip_pass(r1, *right, stepper(r0, r["ar"], r["qr"]))
        return carry

    lax.fori_loop(0, SWEEPS // 2, two_main, 0)
    finish()
    unpack_strips(r["from_left"], r["from_right"], l0, r0)
    lax.fori_loop(0, SWEEPS // 2, two_strips, 0)
    merge_strips(s0, l0, r0)
    second_pass(pert, k_ref, s0, r["gt"], r["inc"], r["place"], norm)
    reduce(
        r["inc"], out, r["total"], r["other"], r["got"], near, anti, pair,
        r["rp_send"], r["rp_recv"], r["r_send"], r["r_recv"],
    )


def body(perturbations, gradient_store, diffusivity, slab_owner):
    members = perturbations.shape[0] * lax.axis_size("member")
    pert = perturbations.reshape(M, SV, NZ, NY, 128)
    grad = gradient_store.reshape(SV * NZ, 128)
    dma = pltpu.SemaphoreType.DMA

    def f32(*shape):
        return pltpu.VMEM(shape + (128,), F32)

    scratch = {
        "pert": pltpu.VMEM(pert.shape, pert.dtype), "pert_sem": dma,
        "full": f32(4 * RING, SV * NZ), "gt": f32(SV * NZ * NY), "pick": f32(NY), "place": f32(NY),
        "s0": f32((NY + 1) * ROW), "s1": f32((NY + 1) * ROW), "kb": f32((NY + 1) * ROW),
        "a": f32(NY * ROW), "q": f32(NY * ROW),
        **{n: f32(9 * ROW) for n in ("l0", "l1", "r0", "r1")},
        **{n: f32(8 * ROW) for n in ("al", "ql", "ar", "qr")},
        **{n: f32(NZ, 8) for n in ("kl", "kr", "hl", "hr")},
        **{n: f32(4 * ROW) for n in ("to_left", "to_right", "from_left", "from_right")},
        "inc": f32(NY * SV * NZ),
        **{n: f32(2 * RING, SV * NZ) for n in ("total", "other", "got")},
        **{n: dma((2, 8)) for n in ("y_send", "y_recv")},
        **{n: dma((18,)) for n in ("p_send", "p_recv")},
        **{n: dma((5,)) for n in ("z_send", "z_recv")},
        "local_sem": dma,
        **{n: dma((2,)) for n in ("h_send", "h_recv", "s_send", "s_recv")},
        **{n: dma((16,)) for n in ("rp_send", "rp_recv", "r_send", "r_recv")},
    }
    out = pl.pallas_call(
        functools.partial(kernel, norm=1.0 / (members - 1), names=tuple(scratch)),
        out_shape=jax.ShapeDtypeStruct((SV * NZ, 128), F32),
        in_specs=[SMEM, VMEM, VMEM, pl.BlockSpec(memory_space=pl.ANY)],
        out_specs=VMEM,
        scratch_shapes=list(scratch.values()),
        compiler_params=pltpu.CompilerParams(vmem_limit_bytes=LIMIT, collective_id=0, has_side_effects=True),
    )(slab_owner, grad, diffusivity, pert)
    return out.reshape(gradient_store.shape)


def solution(mesh):
    in_specs = (
        P("member", None, None, None, None, "tile"),
        P(None, None, None, "member", "tile"),
        P(None, None, "tile"),
        P(),
    )
    out_specs = P(None, None, None, "member", "tile")
    return jax.shard_map(body, mesh=mesh, in_specs=in_specs, out_specs=out_specs, check_vma=False)
```

time: 112 us -> 86.7 us (0.77)
  Pallas kernels: 108 us -> 83.8 us
  other arithmetic: 1.35 us -> 0 us
    pallas_call x7 -> x1, Pallas kernels: 108 us -> 83.8 us  [body(): pl.pallas_call(functools.partial(kernel, norm=1.0 / (members - 1), names=...]
    reduce_sum x1 -> x0, other arithmetic: 1.35 us -> none  [body(): jnp.sum(jnp.where(slab_owner[None, :] == own[:, None], own[None, :], 0),...]
where the time goes in v2:
time: 86.7 us; the launch traced here: 85.2 us
  Pallas kernels  83.8 us (97%)
  local copies, waits for them, and re-layouts  1.4 us (2%)
    pallas_call x1, Pallas kernels, body(): pl.pallas_call(functools.partial(kernel, norm=1.0 / (members - 1), names=...  83.8 us

profile of v2, /device:TPU:6, one launch (start us, length us, event | category | flops | bytes accessed | tf_op | source)
XLA Modules:
  0.0 85.2 jit_solution(2644560452729316144)
XLA Ops:
  0.0 83.8 %shard_map.46 = f32[80,128]{1,0:T(8,128)} custom-call(s32[32]{0:T(128)} %owner.1, f32[80,128]{1,0:T(8,128)} %bitcast.7, f32[8,32,128]{2,1,0:T(8,128)} %k_ref.1, bf16[8,10,8,32,128]{4,3,2,1,0:T(8,128)(2,1)} %bitcast.5), custom_call_target="tpu_custom_call" | custom-call | tf_op jit(solution)/shard_map/pallas_call | solution.py:602
  83.8 1.4 %copy.7 = f32[2,5,8,1,128]{4,3,2,1,0:T(1,128)} copy(f32[2,5,8,1,128]{4,3,2,1,0:T(1,128)} %bitcast.6) | data formatting | bytes 81920

commit v3 on v2

--- a/solution.py
+++ b/solution.py
@@ -44,29 +44,32 @@
     return pl.ds(y * ROW if isinstance(y, int) else pl.multiple_of(y * ROW, ROW), ROW)
 
 
-def rows_pass(src, count, first, p0, pu, emit, unroll):
+def rows_pass(src, count, first, p0, pu, beside, emit, unroll):
     def body(y, carry):
-        p0, pu, cur, side = carry
+        p0, pu, cur = carry
         nxt = src[row_at(y + 1), :]
-        beside = sideways(nxt)
         u = up(nxt, cur)
         four = u + jnp.concatenate([p0, pu[: ROW - M]], axis=0)
-        emit(row_at(y), cur, four + side)
-        return cur[:M], u, nxt, beside
-
-    lax.fori_loop(0, count, body, (p0, pu, first, sideways(first)), unroll=unroll)
-
-
-def main_pass(src, emit, unroll=UNROLL):
+        emit(row_at(y), cur, four + beside(row_at(y), cur))
+        return cur[:M], u, nxt
+
+    lax.fori_loop(0, count, body, (p0, pu, first), unroll=unroll)
+
+
+def rotated(rows, cur):
+    return sideways(cur)
+
+
+def main_pass(src, beside, emit, unroll=UNROLL):
     first = src[row_at(0), :]
-    rows_pass(src, NY, first, jnp.zeros((M, 128), F32), first, emit, unroll)
-
-
-def strip_pass(src, lo, hi, emit, unroll=UNROLL):
+    rows_pass(src, NY, first, jnp.zeros((M, 128), F32), first, beside, emit, unroll)
+
+
+def strip_pass(src, lo, hi, beside, emit, unroll=UNROLL):
     first, last = src[row_at(0), :], src[row_at(7), :]
     prev = jnp.where(lo, 0.0, roll(last, 32))
     src[row_at(8), :] = jnp.where(hi, 0.0, roll(first, 96))
-    rows_pass(src, 8, first, prev[:M], up(first, prev), emit, unroll)
+    rows_pass(src, 8, first, prev[:M], up(first, prev), beside, emit, unroll)
 
 
 def strip_masks():
@@ -82,16 +85,74 @@
         dst_q[rows, :] = cur * cur
 
     if strip is None:
-        main_pass(src, emit)
+        main_pass(src, rotated, emit, 4)
     else:
-        strip_pass(src, *strip, emit)
-
-
-def stepper(dst, a, q):
-    def emit(rows, cur, total):
-        dst[rows, :] = a[rows, :] * cur + q[rows, :] * total
-
-    return emit
+        strip_pass(src, *strip, rotated, emit, 4)
+
+
+def parts(value):
+    high = value.astype(jnp.bfloat16)
+    return high, (value - high.astype(F32)).astype(jnp.bfloat16)
+
+
+def pair_sums(value, ring):
+    return jnp.dot(jnp.concatenate(parts(value), axis=1), ring[...], preferred_element_type=F32)
+
+
+def ring_matrix(ring):
+    row, col = (lax.broadcasted_iota(jnp.int32, (256, 128), i) for i in range(2))
+    apart = (row - col + 128) % 128
+    ring[...] = jnp.where((apart == 1) | (apart == 127), 1.0, 0.0).astype(jnp.bfloat16)
+
+
+def advance(field, pairs, new_field, a, q, start, count, carry, keep):
+    p0, pu, cur = carry
+    for i in range(count):
+        y = start + i
+        nxt = field[row_at(y + 1), :]
+        u = up(nxt, cur)
+        total = (u + jnp.concatenate([p0, pu[: ROW - M]], axis=0)) + pairs[row_at(y), :]
+        new = a[row_at(y), :] * cur + q[row_at(y), :] * total
+        new_field[row_at(y), :] = new
+        keep(i, new)
+        p0, pu, cur = cur[:M], u, nxt
+    return p0, pu, cur
+
+
+CHUNK = 4
+CHUNKS = 8
+
+
+def main_sweep(src, dst, a, q, ring):
+    (field, pairs), (new_field, new_pairs) = src, dst
+
+    def body(i, carry):
+        for n in range(CHUNKS):
+            y, news = (i * CHUNKS + n) * CHUNK, []
+            carry = advance(field, pairs, new_field, a, q, y, CHUNK, carry, lambda i, new: news.append(new))
+            rows = pl.ds(pl.multiple_of(y * ROW, CHUNK * ROW), CHUNK * ROW)
+            value = jnp.concatenate(news, axis=0)
+            new_pairs[rows, :] = sideways(value) if n % 3 == 1 else pair_sums(value, ring)
+        return carry
+
+    first = field[row_at(0), :]
+    lax.fori_loop(0, NY // (CHUNKS * CHUNK), body, (jnp.zeros((M, 128), F32), first, first))
+
+
+def strip_sweeps(sides, ring):
+    starts = []
+    for (field, pairs), dst, a, q, (lo, hi) in sides:
+        first, last = field[row_at(0), :], field[row_at(7), :]
+        prev = jnp.where(lo, 0.0, roll(last, 32))
+        field[row_at(8), :] = jnp.where(hi, 0.0, roll(first, 96))
+        starts.append((prev[:M], up(first, prev), first))
+    for half in range(8 // CHUNK):
+        for n, ((field, pairs), (new_field, new_pairs), a, q, masks) in enumerate(sides):
+            news = []
+            starts[n] = advance(
+                field, pairs, new_field, a, q, half * CHUNK, CHUNK, starts[n], lambda i, new: news.append(new)
+            )
+            new_pairs[pl.ds(half * CHUNK * ROW, CHUNK * ROW), :] = pair_sums(jnp.concatenate(news, axis=0), ring)
 
 
 def k_strips(k_ref, left_ref, right_ref):
@@ -206,7 +267,7 @@
     return ref if part == 0 else ref.at[pl.ds(0 if part == 1 else half, half)]
 
 
-def gather(grad, full, near, anti, pair, y_send, y_recv, p_send, p_recv, z_send, z_recv, local_sem, between):
+def gather(grad, full, near, anti, pair, y_send, y_recv, p_send, p_recv, z_send, z_recv, local_sem, gt, between):
     zh, y, c = here()
     started = []
 
@@ -260,14 +321,36 @@
         send(y_copy(1, kind))
     send(p_copy(1, -1, c))
     between[1]()
+
+    def unload(side, core, *ds):
+        for d in ds:
+            o = member(zh if side == 0 else 1 - zh, y + d, core)["member"]
+            for sv in range(SV):
+                gt[pl.ds(sv * NZ * NY + o, NZ, stride=NY), :] = full[o, pl.ds(sv * NZ, NZ), :]
+
+    def from_pair(side, *kinds):
+        for kind in kinds:
+            p_copy(side, kind, 1 - c).wait_recv()
+
+    mine.wait()
+    unload(0, c, 0, 1, -1, 2, -2)
+    unload(1, c, 0)
     arrivals(0, (4, 6, 5, 7))
-    arrivals(1, (0, 2, 1, 3, 4, 6, 5, 7))
-    mine.wait()
+    unload(0, c, 3, -3, 4)
+    arrivals(1, (0, 2, 1, 3))
+    unload(1, c, 1, -1, 2, -2)
+    from_pair(0, -1, 0, 1, 2, 3)
+    unload(0, 1 - c, 0, 1, -1, 2, -2)
+    arrivals(1, (4, 6, 5, 7))
+    unload(1, c, 3, -3, 4)
+    from_pair(0, 4, 5, 6, 7)
+    unload(0, 1 - c, 3, -3, 4)
+    from_pair(1, -1, 0, 1, 2, 3)
+    unload(1, 1 - c, 0, 1, -1, 2, -2)
+    from_pair(1, 4, 5, 6, 7)
+    unload(1, 1 - c, 3, -3, 4)
     for op in started:
         op.wait_send()
-    for side in range(2):
-        for kind in range(-1, 8):
-            p_copy(side, kind, 1 - c).wait_recv()
 
 
 def selectors(owner, pick, place):
@@ -292,13 +375,7 @@
     return out[:, :128], out[:, 128:]
 
 
-def weigh(pick, full, pert, k_ref, state, gt):
-    def regroup(o, carry):
-        for sv in range(SV):
-            gt[pl.ds(sv * NZ * NY + o, NZ, stride=NY), :] = full[o, pl.ds(sv * NZ, NZ), :]
-        return carry
-
-    lax.fori_loop(0, NY, regroup, 0)
+def weigh(pick, pert, k_ref, state, gt):
     selector = pick[:, pl.ds(0, 2 * NY)].astype(jnp.bfloat16)
 
     def reorder(z, carry):
@@ -329,11 +406,15 @@
     lax.fori_loop(0, 2 * NZ, body, 0)
 
 
-def cut_strips(state, vl, vr):
+def cut_strips(state, pairs, vl, vr, ring):
     region = lanes(ROW) // 32
 
     def body(y, carry):
-        turned = [roll(state[pl.ds(pl.multiple_of((8 * h + y) * ROW, ROW), ROW), :], 32 * h) for h in range(4)]
+        quarters = [state[row_at(8 * h + y), :] for h in range(4)]
+        turned = [roll(row, 32 * h) for h, row in enumerate(quarters)]
+        sums = pair_sums(jnp.concatenate(quarters, axis=0), ring)
+        for h in range(4):
+            pairs[row_at(8 * h + y), :] = sums[h * ROW : (h + 1) * ROW]
         left, right = turned[0], turned[0]
         for h in range(1, 4):
             left = jnp.where(region == h, turned[h], left)
@@ -364,7 +445,7 @@
     lax.fori_loop(0, 8, body, 0)
 
 
-def unpack_strips(from_left, from_right, vl, vr):
+def unpack_strips(from_left, from_right, vl, vr, lp, rp, ring):
     lane = lanes(ROW) % 32
 
     def mixed(even, odd):
@@ -374,8 +455,13 @@
         rows = pl.ds(pl.multiple_of(y * ROW, ROW), ROW)
         packed = pl.ds(pl.multiple_of(y * ROW // 2, ROW // 2), ROW // 2)
         left, right = from_left[packed, :], from_right[packed, :]
-        vl[rows, :] = jnp.where(lane >= 22, mixed(left, roll(left, 10)), vl[rows, :])
-        vr[rows, :] = jnp.where(lane < 10, mixed(right, roll(right, 118)), vr[rows, :])
+        left = jnp.where(lane >= 22, mixed(left, roll(left, 10)), vl[rows, :])
+        right = jnp.where(lane < 10, mixed(right, roll(right, 118)), vr[rows, :])
+        vl[rows, :] = left
+        vr[rows, :] = right
+        sums = pair_sums(jnp.concatenate([left, right], axis=0), ring)
+        lp[rows, :] = sums[:ROW]
+        rp[rows, :] = sums[ROW:]
         return carry
 
     lax.fori_loop(0, 8, body, 0)
@@ -525,6 +611,7 @@
     kb, halos = r["kb"], []
 
     def first():
+        ring_matrix(r["ring"])
         k_strips(k_ref, r["kl"], r["kr"])
         halos.append(halo_start(r["kl"], r["kr"], r["hl"], r["hr"], r["h_send"], r["h_recv"]))
         kb[row_at(NY), :] = jnp.zeros((ROW, 128), F32)
@@ -540,29 +627,34 @@
 
     gather(
         grad, r["full"], near, anti, pair, r["y_send"], r["y_recv"], r["p_send"], r["p_recv"], r["z_send"], r["z_recv"],
-        r["local_sem"], (first, second),
+        r["local_sem"], r["gt"], (first, second),
     )
     fetch.wait()
-    weigh(r["pick"], r["full"], pert, k_ref, s0, r["gt"])
-    cut_strips(s0, l0, r0)
+    weigh(r["pick"], pert, k_ref, s0, r["gt"])
+    cut_strips(s0, r["sp0"], l0, r0, r["ring"])
     pack_strips(l0, r0, r["to_left"], r["to_right"])
     finish = halo_start(r["to_left"], r["to_right"], r["from_left"], r["from_right"], r["s_send"], r["s_recv"])
 
+    main = ((s0, r["sp0"]), (s1, r["sp1"]))
+    lefts = ((l0, r["lp0"]), (l1, r["lp1"]))
+    rights = ((r0, r["rp0"]), (r1, r["rp1"]))
+
     def two_main(i, carry):
-        main_pass(s0, stepper(s1, r["a"], r["q"]))
-        main_pass(s1, stepper(s0, r["a"], r["q"]))
+        for n in range(2):
+            main_sweep(main[n], main[1 - n], r["a"], r["q"], r["ring"])
         return carry
 
     def two_strips(i, carry):
-        strip_pass(l0, *left, stepper(l1, r["al"], r["ql"]))
-        strip_pass(r0, *right, stepper(r1, r["ar"], r["qr"]))
-        strip_pass(l1, *left, stepper(l0, r["al"], r["ql"]))
-        strip_pass(r1, *right, stepper(r0, r["ar"], r["qr"]))
+        for n in range(2):
+            strip_sweeps(
+                ((lefts[n], lefts[1 - n], r["al"], r["ql"], left), (rights[n], rights[1 - n], r["ar"], r["qr"], right)),
+                r["ring"],
+            )
         return carry
 
     lax.fori_loop(0, SWEEPS // 2, two_main, 0)
     finish()
-    unpack_strips(r["from_left"], r["from_right"], l0, r0)
+    unpack_strips(r["from_left"], r["from_right"], l0, r0, r["lp0"], r["rp0"], r["ring"])
     lax.fori_loop(0, SWEEPS // 2, two_strips, 0)
     merge_strips(s0, l0, r0)
     second_pass(pert, k_ref, s0, r["gt"], r["inc"], r["place"], norm)
@@ -585,9 +677,10 @@
         "pert": pltpu.VMEM(pert.shape, pert.dtype), "pert_sem": dma,
         "full": f32(4 * RING, SV * NZ), "gt": f32(SV * NZ * NY), "pick": f32(NY), "place": f32(NY),
         "s0": f32((NY + 1) * ROW), "s1": f32((NY + 1) * ROW), "kb": f32((NY + 1) * ROW),
-        "a": f32(NY * ROW), "q": f32(NY * ROW),
+        **{n: f32(NY * ROW) for n in ("a", "q", "sp0", "sp1")},
+        "ring": pltpu.VMEM((256, 128), jnp.bfloat16),
         **{n: f32(9 * ROW) for n in ("l0", "l1", "r0", "r1")},
-        **{n: f32(8 * ROW) for n in ("al", "ql", "ar", "qr")},
+        **{n: f32(8 * ROW) for n in ("al", "ql", "ar", "qr", "lp0", "lp1", "rp0", "rp1")},
         **{n: f32(NZ, 8) for n in ("kl", "kr", "hl", "hr")},
         **{n: f32(4 * ROW) for n in ("to_left", "to_right", "from_left", "from_right")},
         "inc": f32(NY * SV * NZ),

time: 86.7 us -> 69.4 us (0.80); the launches traced: 85.2 us -> 69.2 us
  Pallas kernels: 83.8 us -> 67.8 us
    pallas_call x1, Pallas kernels: 83.8 us -> 67.8 us  [body(): pl.pallas_call(functools.partial(kernel, norm=1.0 / (members - 1), names=...]
where the time goes in v3:
time: 69.4 us; the launch traced here: 69.2 us
  Pallas kernels  67.8 us (98%)
  local copies, waits for them, and re-layouts  1.4 us (2%)
    pallas_call x1, Pallas kernels, body(): pl.pallas_call(functools.partial(kernel, norm=1.0 / (members - 1), names=...  67.8 us
    unnamed x1, local copies, waits for them, and re-layouts  1.4 us

profile of v3, /device:TPU:6, one launch (start us, length us, event | category | flops | bytes accessed | tf_op | source)
XLA Modules:
  0.0 69.2 jit_solution(872282428794412732)
XLA Ops:
  0.0 67.8 %shard_map.46 = f32[80,128]{1,0:T(8,128)} custom-call(s32[32]{0:T(128)} %owner.1, f32[80,128]{1,0:T(8,128)} %bitcast.7, f32[8,32,128]{2,1,0:T(8,128)} %k_ref.1, bf16[8,10,8,32,128]{4,3,2,1,0:T(8,128)(2,1)} %bitcast.5), custom_call_target="tpu_custom_call" | custom-call | tf_op jit(solution)/shard_map/pallas_call | solution.py:695
  67.8 1.4 %copy.7 = f32[2,5,8,1,128]{4,3,2,1,0:T(1,128)} copy(f32[2,5,8,1,128]{4,3,2,1,0:T(1,128)} %bitcast.6) | data formatting | bytes 81920

commit v4 on v3

--- a/solution.py
+++ b/solution.py
@@ -385,11 +385,9 @@
                 gt[place, :] = value
         return carry
 
-    lax.fori_loop(0, NZ, reorder, 0)
-
-    def body(i, carry):
-        z, b = i // 2, lax.rem(i, 2)
-        y0 = pl.multiple_of(b * 16, 16)
+    lax.fori_loop(0, NZ, reorder, 0, unroll=4)
+
+    def body(z, carry, y0):
         grads = [gt[pl.ds(pl.multiple_of(sv * NZ * NY + z * NY + y0, 16), 16), :] for sv in range(SV)]
         k = k_ref[z, pl.ds(y0, 16), :]
         for m in range(M):
@@ -403,7 +401,8 @@
                 state[pl.ds(start, 8, stride=ROW), :] = total[8 * part : 8 * part + 8]
         return carry
 
-    lax.fori_loop(0, 2 * NZ, body, 0)
+    for y0 in (0, 16):
+        lax.fori_loop(0, NZ, functools.partial(body, y0=y0), 0)
 
 
 def cut_strips(state, pairs, vl, vr, ring):
@@ -424,7 +423,7 @@
         vr[rows, :] = right
         return carry
 
-    lax.fori_loop(0, 8, body, 0)
+    lax.fori_loop(0, 8, body, 0, unroll=4)
 
 
 def evens(row, odd):
@@ -442,7 +441,7 @@
         to_left[out, :] = jnp.where(lane < 10, evens(left, 0), roll(evens(left, 1), 10))
         return carry
 
-    lax.fori_loop(0, 8, body, 0)
+    lax.fori_loop(0, 8, body, 0, unroll=4)
 
 
 def unpack_strips(from_left, from_right, vl, vr, lp, rp, ring):
@@ -464,7 +463,7 @@
         rp[rows, :] = sums[ROW:]
         return carry
 
-    lax.fori_loop(0, 8, body, 0)
+    lax.fori_loop(0, 8, body, 0, unroll=4)
 
 
 def merge_strips(state, vl, vr):
@@ -479,13 +478,11 @@
             state[place, :] = jnp.where(inner, state[place, :], roll(edge, -32 * h))
         return carry
 
-    lax.fori_loop(0, 8, body, 0)
+    lax.fori_loop(0, 8, body, 0, unroll=4)
 
 
 def second_pass(pert, k_ref, state, natural, inc, place, norm):
-    def body(i, carry):
-        z, b = i // 2, lax.rem(i, 2)
-        y0 = pl.multiple_of(b * 16, 16)
+    def body(z, carry, y0):
         factor = norm / k_ref[z, pl.ds(y0, 16), :]
         local = []
         for m in range(M):
@@ -499,7 +496,8 @@
             natural[pl.ds(pl.multiple_of(sv * NZ * NY + z * NY + y0, 16), 16), :] = total * factor
         return carry
 
-    lax.fori_loop(0, 2 * NZ, body, 0)
+    for y0 in (0, 16):
+        lax.fori_loop(0, NZ, functools.partial(body, y0=y0), 0)
     selector = place[:, pl.ds(0, 2 * NY)].astype(jnp.bfloat16)
 
     def reorder(z, carry):
@@ -510,7 +508,7 @@
                     inc[pl.ds(d8 * SV * NZ + (sv + i) * NZ + z, 8, stride=SV * NZ), :] = value[d8 : d8 + 8]
         return carry
 
-    lax.fori_loop(0, NZ, reorder, 0)
+    lax.fori_loop(0, NZ, reorder, 0, unroll=4)
 
 
 def reduce(inc, out, total, other, got, near, anti, pair, p_send, p_recv, send_sem, recv_sem):

time: 69.4 us -> 64.9 us (0.935)
  Pallas kernels: 67.8 us -> 63.3 us
    pallas_call x1, Pallas kernels: 67.8 us -> 63.3 us  [body(): pl.pallas_call(functools.partial(kernel, norm=1.0 / (members - 1), names=...]
where the time goes in v4:
time: 64.9 us; the launch traced here: 64.7 us
  Pallas kernels  63.3 us (98%)
  local copies, waits for them, and re-layouts  1.4 us (2%)
    pallas_call x1, Pallas kernels, body(): pl.pallas_call(functools.partial(kernel, norm=1.0 / (members - 1), names=...  63.3 us
    unnamed x1, local copies, waits for them, and re-layouts  1.4 us

profile of v4, /device:TPU:6, one launch (start us, length us, event | category | flops | bytes accessed | tf_op | source)
XLA Modules:
  0.0 64.7 jit_solution(8984506078906297123)
XLA Ops:
  0.0 63.3 %shard_map.46 = f32[80,128]{1,0:T(8,128)} custom-call(s32[32]{0:T(128)} %owner.1, f32[80,128]{1,0:T(8,128)} %bitcast.7, f32[8,32,128]{2,1,0:T(8,128)} %k_ref.1, bf16[8,10,8,32,128]{4,3,2,1,0:T(8,128)(2,1)} %bitcast.5), custom_call_target="tpu_custom_call" | custom-call | tf_op jit(solution)/shard_map/pallas_call | solution.py:693
  63.3 1.4 %copy.7 = f32[2,5,8,1,128]{4,3,2,1,0:T(1,128)} copy(f32[2,5,8,1,128]{4,3,2,1,0:T(1,128)} %bitcast.6) | data formatting | bytes 81920
